TPU v7x, 32 devices: a whole 2x2x4 slice. The times are simulated.
32 devices in a mesh: ctx: 8 (over z, x), tp: 4 (over y, core).
Axes of the slice: x: 2, y: 2, z: 4, core: 2. Of those that a mesh axis runs over, the one named last changes fastest.
Arguments:
- mel_frames: bfloat16 [65536, 128], P(('ctx', 'tp')), may hold values from -6 to 6
- utterance_ids: int32 [32, 256], P(('ctx', 'tp')), may hold values from 0 to 15, never falling along the last dimension, each value on 1 to 128 neighbouring positions
- frame_counts: int32 [32, 8], replicated, may hold values from 16 to 48, as said below
- input_proj: bfloat16 [128, 256], replicated, may hold values from -0.75 to 0.75
- sub_depthwise: bfloat16 [3, 2, 256], replicated, may hold values from -4 to 4
- sub_pointwise: bfloat16 [3, 256, 256], replicated, may hold values from -0.5 to 0.5
- output_proj: bfloat16 [256, 1024], replicated, may hold values from -0.375 to 0.375
- norm_gain: bfloat16 [1024], replicated, may hold values from 0.099609375 to 1.8984375
- pointwise_one: bfloat16 [1024, 2048], replicated, may hold values from -0.1875 to 0.1875
- depthwise_taps: bfloat16 [9, 1024], replicated, may hold values from -3.5 to 3.5
- pointwise_two: bfloat16 [1024, 1024], replicated, may hold values from -0.1875 to 0.1875
- projector: bfloat16 [1024, 2048], P('tp'), may hold values from -0.1875 to 0.1875
- embed_grads: bfloat16 [8192, 2048], P(('ctx', 'tp')), may hold values from -0.15625 to 0.15625
Outputs:
- llm_embed: bfloat16 [8192, 2048], P(('ctx', 'tp'))
- projector_grad: float32 [1024, 2048], P('tp', 'ctx')
- pointwise_one_grad: float32 [1024, 2048], P(None, ('ctx', 'tp'))
- pointwise_two_grad: float32 [1024, 1024], P(None, ('ctx', 'tp'))
Inputs may be any that keep to these rules, and one draw needn't show every extreme that they name: frame_counts[d, c] is 32 plus or minus 256 / 16; the sign is a sign of pack d times a sign of shard c, and each kind of sign is positive for exactly half of the packs or shards. So every row sums to 256, every column to 1024, and the largest count is 48.
All inputs are finite; a program needn't handle non-finite values.
Results may differ from a plain program's by a relative error of at most 0.028.
Values may be sent and summed in bfloat16 or wider, within the bound.
A program may use at most 128 MiB of HBM per device.

v0:
```python
import jax
import jax.numpy as jnp
from jax import lax
from jax.sharding import PartitionSpec as P


def exchange(value, axis_name, flip):
    size = lax.axis_size(axis_name)
    return lax.ppermute(value, axis_name, [(rank, rank ^ flip) for rank in range(size)])


def axis_bits(axis_name):
    return lax.axis_size(axis_name).bit_length() - 1


def gather_blocks(block, axis_name):
    blocks = {0: block}
    for bit in reversed(range(axis_bits(axis_name))):
        for flip, held in list(blocks.items()):
            blocks[flip ^ (1 << bit)] = exchange(held, axis_name, 1 << bit)
    return [blocks[flip] for flip in range(lax.axis_size(axis_name))]


def fold_scatter(value, order, dims, last=False):
    layout = sorted(dims, key=lambda step: (step[0] != "ctx", -step[1]))
    for position, step in enumerate(order):
        axis_name, bit = step
        dim = layout.index(step)
        layout.remove(step)
        mine = (lax.axis_index(axis_name) >> bit) & 1
        keep = lax.dynamic_index_in_dim(value, mine, dim, keepdims=False)
        send = lax.dynamic_index_in_dim(value, 1 - mine, dim, keepdims=False)
        came = exchange(send, axis_name, 1 << bit)
        value = keep.astype(jnp.float32) + came.astype(jnp.float32)
        if not last or position + 1 < len(order):
            value = value.astype(jnp.bfloat16)
    return value


def split_bits(value, steps):
    return value.reshape((2,) * steps + (value.shape[0] >> steps,) + value.shape[1:])


def subsample(frames_in, input_proj, sub_depthwise, sub_pointwise, output_proj):
    encoded_rows = frames_in.shape[0] // 8
    channels = input_proj.shape[1]
    by_phase = frames_in.reshape(encoded_rows, 8, frames_in.shape[1]).transpose(1, 0, 2)
    hidden = jax.nn.relu(
        jnp.dot(
            by_phase.reshape(8 * encoded_rows, frames_in.shape[1]),
            input_proj,
            preferred_element_type=jnp.float32,
        )
    ).astype(jnp.bfloat16)
    length = 8
    for section_index in range(3):
        length = length // 2
        grouped = hidden.reshape(length, 2, encoded_rows, channels).astype(jnp.float32)
        tap_pair = sub_depthwise[section_index].astype(jnp.float32)
        strided = (grouped[:, 0] * tap_pair[0] + grouped[:, 1] * tap_pair[1]).astype(jnp.bfloat16)
        hidden = jax.nn.relu(
            jnp.dot(
                strided.reshape(length * encoded_rows, channels),
                sub_pointwise[section_index],
                preferred_element_type=jnp.float32,
            )
        ).astype(jnp.bfloat16)
    return jnp.dot(hidden, output_proj, preferred_element_type=jnp.float32)


def depthwise(values, segments, kernel):
    row_total = values.shape[0]
    padded = jnp.pad(values, ((4, 4), (0, 0)))
    padded_ids = jnp.pad(segments, 4, constant_values=-1)
    running_sum = jnp.zeros(values.shape, jnp.float32)
    for tap_index in range(9):
        same_utt = (padded_ids[tap_index : tap_index + row_total] == segments).astype(jnp.float32)[
            :, None
        ]
        running_sum = (
            running_sum + kernel[tap_index] * padded[tap_index : tap_index + row_total] * same_utt
        )
    return running_sum


def depthwise_back(grad_rows, segments, kernel):
    row_total = grad_rows.shape[0]
    padded_ids = jnp.pad(segments, 4, constant_values=-1)
    running_sum = jnp.zeros(grad_rows.shape, jnp.float32)
    for tap_index in range(9):
        same_utt = (padded_ids[tap_index : tap_index + row_total] == segments).astype(jnp.float32)[
            :, None
        ]
        moved_rows = jnp.pad(grad_rows * same_utt, ((4, 4), (0, 0)))
        running_sum = (
            running_sum + kernel[tap_index] * moved_rows[8 - tap_index : 8 - tap_index + row_total]
        )
    return running_sum


def conv_forward(inputs, segments, norm_gain, pointwise_one, depthwise_taps, pointwise_two):
    center = jnp.mean(inputs, axis=1, keepdims=True)
    spread = jnp.mean(jnp.square(inputs - center), axis=1, keepdims=True)
    normed = ((inputs - center) * lax.rsqrt(spread + 1e-05) * norm_gain.astype(jnp.float32)).astype(
        jnp.bfloat16
    )
    raised = jnp.dot(normed, pointwise_one, preferred_element_type=jnp.float32)
    model_width = inputs.shape[1]
    gated_rows = raised[:, :model_width] * jax.nn.sigmoid(raised[:, model_width:])
    mixed_rows = depthwise(gated_rows, segments, depthwise_taps.astype(jnp.float32))
    activated = (mixed_rows * jax.nn.sigmoid(mixed_rows)).astype(jnp.bfloat16)
    output = (
        inputs + jnp.dot(activated, pointwise_two, preferred_element_type=jnp.float32)
    ).astype(jnp.bfloat16)
    return (output, (normed, raised, mixed_rows, activated))


def raised_backward(output_grad, segments, depthwise_taps, pointwise_two, kept_state):
    _, raised, mixed_rows, _ = kept_state
    model_width = output_grad.shape[1]
    act_grad = lax.dot_general(
        output_grad,
        pointwise_two,
        (((1,), (1,)), ((), ())),
        preferred_element_type=jnp.float32,
    )
    sigmoid_mix = jax.nn.sigmoid(mixed_rows)
    mixed_grad = act_grad * (sigmoid_mix + mixed_rows * sigmoid_mix * (1.0 - sigmoid_mix))
    gated_grad = depthwise_back(mixed_grad, segments, depthwise_taps.astype(jnp.float32))
    sigmoid_gate = jax.nn.sigmoid(raised[:, model_width:])
    return jnp.concatenate(
        [
            gated_grad * sigmoid_gate,
            gated_grad * raised[:, :model_width] * sigmoid_gate * (1.0 - sigmoid_gate),
        ],
        axis=1,
    ).astype(jnp.bfloat16)


def rows_product(left, right):
    return lax.dot_general(
        left, right, (((0,), (0,)), ((), ())), preferred_element_type=jnp.float32
    )


def pick(wanted, slots, rows):
    chosen = (wanted[:, None] == slots[None, :]).astype(jnp.bfloat16)
    return jnp.dot(chosen, rows, preferred_element_type=jnp.float32).astype(jnp.bfloat16)


def body(
    mel_frames,
    utterance_ids,
    frame_counts,
    input_proj,
    sub_depthwise,
    sub_pointwise,
    output_proj,
    norm_gain,
    pointwise_one,
    depthwise_taps,
    pointwise_two,
    projector,
    embed_grads,
):
    ctx_count = lax.axis_size("ctx")
    tp_count = lax.axis_size("tp")
    device_count = ctx_count * tp_count
    ctx_rank = lax.axis_index("ctx")
    tp_rank = lax.axis_index("tp")
    my_device = ctx_rank * tp_count + tp_rank
    segments = utterance_ids[0]
    encoded_rows = mel_frames.shape[0] // 8
    model_width = output_proj.shape[1]
    feature_part = model_width // tp_count
    slot_count = 3 * encoded_rows // (2 * ctx_count)
    ctx_steps = [("ctx", bit) for bit in range(axis_bits("ctx"))]
    tp_steps = [("tp", bit) for bit in range(axis_bits("tp"))]
    near, far = tp_steps[:1], tp_steps[1:]
    step_count = len(ctx_steps) + len(tp_steps)

    slot_index = jnp.arange(slot_count, dtype=jnp.int32)
    shard_id = jnp.arange(ctx_count, dtype=jnp.int32)
    pack_id = jnp.arange(device_count, dtype=jnp.int32)
    my_counts = lax.dynamic_index_in_dim(frame_counts, my_device, 0, keepdims=False)
    my_starts = jnp.sum(jnp.where(shard_id[None, :] < shard_id[:, None], my_counts[None, :], 0), 1)
    row_of_slot = jnp.where(
        slot_index[None, :] < my_counts[:, None], my_starts[:, None] + slot_index[None, :], -1
    ).reshape(-1)
    shard_counts = lax.dynamic_index_in_dim(frame_counts, ctx_rank, 1, keepdims=False)
    shard_starts = jnp.sum(
        jnp.where(pack_id[None, :] < pack_id[:, None], shard_counts[None, :], 0), 1
    )
    place_of_slot = jnp.where(
        slot_index[None, :] < shard_counts[:, None],
        shard_starts[:, None] + slot_index[None, :],
        -1,
    )
    place_of_slot = (
        place_of_slot.reshape(ctx_count, tp_count, slot_count).transpose(1, 0, 2).reshape(-1)
    )
    local_rows = jnp.arange(encoded_rows, dtype=jnp.int32)
    places = [(tp_rank ^ flip) * encoded_rows + local_rows for flip in range(tp_count)]

    def spread(values):
        return lax.all_to_all(
            values.reshape(device_count, slot_count, feature_part),
            ("tp", "ctx"),
            split_axis=0,
            concat_axis=0,
            tiled=True,
        )

    cot_blocks = gather_blocks(embed_grads, "tp")
    frame_back = jnp.concatenate(
        [
            lax.dot_general(
                cot, projector, (((1,), (1,)), ((), ())), preferred_element_type=jnp.float32
            ).astype(jnp.bfloat16)
            for cot in cot_blocks
        ]
    )
    parcel = pick(place_of_slot, jnp.concatenate(places), frame_back)
    returned = spread(parcel)
    late_projector, _ = lax.optimization_barrier((projector, cot_blocks[-1]))
    projector_blocks = gather_blocks(late_projector, "tp")

    inputs = subsample(mel_frames, input_proj, sub_depthwise, sub_pointwise, output_proj)
    encoded, kept_state = conv_forward(
        inputs, segments, norm_gain, pointwise_one, depthwise_taps, pointwise_two
    )
    normed, _, _, activated = kept_state
    encoded, _ = lax.optimization_barrier((encoded, parcel))
    outgoing = jnp.concatenate(
        [pick(row_of_slot, local_rows, part) for part in jnp.split(encoded, tp_count, axis=1)]
    )
    returned, outgoing = lax.optimization_barrier((returned, outgoing))
    arrived = spread(outgoing).reshape(device_count * slot_count, feature_part)

    returned = returned.reshape(tp_count, ctx_count * slot_count, feature_part)
    output_grad = jnp.concatenate(
        [pick(local_rows, row_of_slot, returned[part]) for part in range(tp_count)], axis=1
    )
    two_grad = rows_product(output_grad, activated).astype(jnp.bfloat16)
    raised_grad = raised_backward(output_grad, segments, depthwise_taps, pointwise_two, kept_state)
    one_grad = rows_product(raised_grad, normed).astype(jnp.bfloat16)
    one_near = fold_scatter(split_bits(one_grad, step_count), near, ctx_steps + tp_steps)
    two_near = fold_scatter(split_bits(two_grad, step_count), near, ctx_steps + tp_steps)
    arrived, _ = lax.optimization_barrier((arrived, one_near))
    rest = ctx_steps + far
    half = one_near.shape[-2] // 2
    parts = [one_near[..., :half, :], one_near[..., half:, :], two_near]
    orders = [ctx_steps + far, ctx_steps[1:] + far + ctx_steps[:1], far + ctx_steps]
    parts = [fold_scatter(part, order[:1], rest) for part, order in zip(parts, orders)]
    after_first = parts[0], parts[1]
    parts = [
        fold_scatter(part, order[1:], [step for step in rest if step != order[0]], last=True)
        for part, order in zip(parts, orders)
    ]
    one_part = jnp.concatenate(parts[:2], axis=0).T
    two_part = parts[2].T

    frame_blocks = [pick(place, place_of_slot, arrived) for place in places]
    weight_sum = sum(rows_product(cot, held) for cot, held in zip(cot_blocks, frame_blocks))
    projector_grad = fold_scatter(
        split_bits(weight_sum.astype(jnp.bfloat16), len(ctx_steps)), ctx_steps, ctx_steps, last=True
    ).T
    row_blocks = [frame_blocks[0]] + [
        exchange(frame_blocks[flip], "tp", flip) for flip in range(1, tp_count)
    ]
    row_blocks, _ = lax.optimization_barrier((row_blocks, after_first))
    llm_embed = sum(
        jnp.dot(held, weights, preferred_element_type=jnp.float32)
        for held, weights in zip(row_blocks, projector_blocks)
    ).astype(jnp.bfloat16)
    return (llm_embed, projector_grad, one_part, two_part)


def solution(mesh):
    placed = (
        P(("ctx", "tp"), None),
        P(("ctx", "tp"), None),
        P(),
        P(),
        P(),
        P(),
        P(),
        P(),
        P(),
        P(),
        P(),
        P("tp", None),
        P(("ctx", "tp"), None),
    )
    return jax.shard_map(
        body,
        mesh=mesh,
        in_specs=placed,
        out_specs=(
            P(("ctx", "tp"), None),
            P("tp", "ctx"),
            P(None, ("ctx", "tp")),
            P(None, ("ctx", "tp")),
        ),
        check_vma=False,
    )
```

profile of v0, /device:TPU:0, one launch (start us, length us, event | category | flops | bytes accessed | tf_op | source)
XLA Modules:
  0.0 206.0 jit_solution(17528383099561901095)
XLA Ops:
  0.6 3.1 %collective-permute-start.1 = (bf16[256,2048]{1,0:T(8,128)(2,1)}, bf16[256,2048]{1,0:T(8,128)(2,1)}, u32[]{:S(2)}, u32[]{:S(2)}) collective-permute-start(bf16[256,2048]{1,0:T(8,128)(2,1)} %param.25), channel_id=1, source_target_pairs={{0,2},{1,3},{2,0},{3,1},{4,6},{5,7},{6,4},{7,5},{8,10},{9,11},{10,... | collective-permute-start | bytes 3145736 | tf_op jit(solution)/shard_map/ppermute | solution.py:9
  14.2 4.9 %fusion.141 = f32[256,2048]{1,0:T(8,128)} fusion(bf16[1024,2048]{1,0:T(8,128)(2,1)} %param.21, f32[256,1024]{1,0:T(8,128)S(1)} %get-tuple-element.73, f32[1024]{0:T(1024)S(1)} %convert_element_type.433, f32[256]{0:T(256)S(1)} %add_rsqrt_fusion, f32[256]{0:T(256)S(1)} %broadcast_multiply_fusion.8), kind=kOutput, calls=%fused_computation.267 | convolution fusion | flops 1074790400 | bytes 7346176 | tf_op jit(solution)/shard_map/dot_general | solution.py:107
  19.2 3.0 %slice_multiply_fusion.2 = f32[256,1024]{1,0:T(8,128)} fusion(f32[256,2048]{1,0:T(8,128)} %fusion.141), kind=kLoop, calls=%fused_computation.120 | loop fusion | flops 1048576 | bytes 3145728 | tf_op jit(solution)/shard_map/mul | solution.py:109
  22.7 4.5 %collective-permute-done.1 = bf16[256,2048]{1,0:T(8,128)(2,1)} collective-permute-done((bf16[256,2048]{1,0:T(8,128)(2,1)}, bf16[256,2048]{1,0:T(8,128)(2,1)}, u32[]{:S(2)}, u32[]{:S(2)}) %collective-permute-start.1) | collective-permute-done | bytes 1048608 | tf_op jit(solution)/shard_map/ppermute | solution.py:9
  27.4 7.6 %multiply_add_fusion = f32[256,1024]{1,0:T(8,128)} fusion(f32[256,1024]{1,0:T(8,128)} %slice_multiply_fusion.2, f32[256]{0:T(256)S(1)} %get-tuple-element.71, f32[1024]{0:T(1024)S(1)} %bitcast.240, f32[256]{0:T(256)S(1)} %get-tuple-element.65, f32[1024]{0:T(1024)S(1)} %bitcast.238, f32[256]{0:T(256)S(1)} %get-tuple-element.66, f32[1024]{0:T(1024)S(1)} %bitcast.236, ...), kind=kLoop, calls=%fused_computation.106 | loop fusion | flops 6553600 | bytes 2142208 | tf_op jit(solution)/shard_map/add | solution.py:81
  40.1 2.1 %fusion.6 = bf16[1536,256]{1,0:T(8,128)(2,1)} fusion(s32[1024]{0:T(1024)S(1)} %pad_add_fusion, s32[1536]{0:T(1024)S(1)} %select_n.112, bf16[256,256]{1,0:T(8,128)(2,1)S(1)} %convolution_convert_fusion.10, bf16[256,256]{1,0:T(8,128)(2,1)S(1)} %convolution_convert_fusion.11, bf16[256,256]{1,0:T(8,128)(2,1)S(1)} %convolution_convert_fusion.12, ...), kind=kOutput, calls=%fused_computation.14 | convolution fusion | flops 809369600 | bytes 1320960 | tf_op jit(solution)/shard_map/dot_general | solution.py:148
  42.2 6.5 %all-to-all-start = ((bf16[32,48,256]{2,1,0:T(8,128)(2,1)}), bf16[32,48,256]{2,1,0:T(8,128)(2,1)}, u32[]{:S(2)}, u32[]{:S(2)}) async-start(bf16[32,48,256]{2,1,0:T(8,128)(2,1)} %bitcast.217), calls=%async_computation | async-start | bytes 1572864 | tf_op jit(solution)/shard_map/all_to_all | solution.py:206
  48.7 2.3 %fusion.22 = bf16[256,1024]{1,0:T(8,128)(2,1)S(1)} fusion(f32[256,1024]{1,0:T(8,128)} %copy-done.7, bf16[1024,1024]{1,0:T(8,128)(2,1)S(1)} %copy-done, f32[256,1024]{1,0:T(8,128)} %multiply_add_fusion), kind=kOutput, calls=%fused_computation.35 | convolution fusion | flops 538705920 | bytes 4718592 | tf_op jit(solution)/shard_map/dot_general | solution.py:113
  52.9 17.4 %all-to-all-done = bf16[32,48,256]{2,1,0:T(8,128)(2,1)} async-done(((bf16[32,48,256]{2,1,0:T(8,128)(2,1)}), bf16[32,48,256]{2,1,0:T(8,128)(2,1)}, u32[]{:S(2)}, u32[]{:S(2)}) %all-to-all-start) | async-done | bytes 786464 | tf_op jit(solution)/shard_map/all_to_all | solution.py:206
  85.2 11.1 %collective-permute-done.22 = bf16[2,2,2,32,1024]{4,3,0,1,2:T(8,128)(2,1)} collective-permute-done((bf16[2,2,2,32,1024]{4,3,0,1,2:T(8,128)(2,1)}, bf16[2,2,2,32,1024]{4,3,0,1,2:T(8,128)(2,1)}, u32[]{:S(2)}, u32[]{:S(2)}) %collective-permute-start.22) | collective-permute-done | bytes 524320 | tf_op jit(solution)/shard_map/ppermute | solution.py:9
  100.3 3.6 %all-to-all-start.1 = ((bf16[32,48,256]{2,1,0:T(8,128)(2,1)}), bf16[32,48,256]{2,1,0:T(8,128)(2,1)}, u32[]{:S(2)}, u32[]{:S(2)}) async-start(bf16[32,48,256]{2,1,0:T(8,128)(2,1)} %bitcast.210), calls=%async_computation.1 | async-start | bytes 1572864 | tf_op jit(solution)/shard_map/all_to_all | solution.py:206
  108.3 11.3 %collective-permute-done.24 = bf16[2,32,1024]{2,1,0:T(8,128)(2,1)} collective-permute-done((bf16[2,32,1024]{2,1,0:T(8,128)(2,1)S(1)}, bf16[2,32,1024]{2,1,0:T(8,128)(2,1)}, u32[]{:S(2)}, u32[]{:S(2)}) %collective-permute-start.24) | collective-permute-done | bytes 131104 | tf_op jit(solution)/shard_map/ppermute | solution.py:9
  120.5 4.8 %collective-permute-start.25 = (bf16[32,1024]{1,0:T(8,128)(2,1)S(1)}, bf16[32,1024]{1,0:T(8,128)(2,1)S(1)}, u32[]{:S(2)}, u32[]{:S(2)}) collective-permute-start(bf16[32,1024]{1,0:T(8,128)(2,1)S(1)} %dynamic-slice_bitcast_fusion.11), channel_id=1, source_target_pairs={{0,16},{4,20},{8,24},{12,28},{16,0},{20,4},{24,8},{28,12},{1,17},{... | collective-permute-start | bytes 196616 | tf_op jit(solution)/shard_map/ppermute | solution.py:9
  125.3 6.4 %collective-permute-done.10 = bf16[256,2048]{1,0:T(8,128)(2,1)} collective-permute-done((bf16[256,2048]{1,0:T(8,128)(2,1)S(1)}, bf16[256,2048]{1,0:T(8,128)(2,1)}, u32[]{:S(2)}, u32[]{:S(2)}) %collective-permute-start.10) | collective-permute-done | bytes 1048608 | tf_op jit(solution)/shard_map/ppermute | solution.py:9
  132.4 2.7 %fusion.2 = bf16[2,2,2,2,64,1024]{5,4,2,3,0,1:T(8,128)(2,1)S(1)} fusion(bf16[2,2,2,2,64,1024]{5,4,2,3,0,1:T(8,128)(2,1)} %collective-permute-done.3, bf16[2,2,2,2,1,64,1024]{6,5,4,3,2,1,0:T(8,128)(2,1)S(1)} %get-tuple-element.24), kind=kLoop, calls=%fused_computation.3 | loop fusion | flops 4194304 | bytes 6291456 | tf_op jit(solution)/shard_map/convert_element_type | solution.py:36
  138.3 2.2 %fusion.29 = bf16[256,256]{1,0:T(8,128)(2,1)} fusion(bf16[1536,256]{1,0:T(8,128)(2,1)} %bitcast.36, s32[1536]{0:T(1024)S(1)} %select_n.112, s32[256]{0:T(256)S(1)} %get-tuple-element.77), kind=kOutput, calls=%fused_computation.50 | convolution fusion | flops 201785344 | bytes 924672 | tf_op jit(solution)/shard_map/dot_general | solution.py:148
  151.3 2.7 %fusion.12 = bf16[2048,256]{0,1:T(8,128)(2,1)} fusion(f32[256,2048]{1,0:T(8,128)S(1)} %convolution_add_fusion.1, bf16[256,256]{1,0:T(8,128)(2,1)S(1)} %fusion.35, bf16[256,2048]{1,0:T(8,128)(2,1)} %collective-permute-done.2), kind=kOutput, calls=%fused_computation.18 | convolution fusion | flops 269484032 | bytes 4325376 | tf_op jit(solution)/shard_map/dot_general | solution.py:141
  155.8 2.2 %constant_dynamic-slice_fusion.3 = (bf16[2,2,1,256,256]{3,2,1,0,4:T(2,128)(2,1)S(1)}, bf16[2,2,1,256,256]{3,2,1,0,4:T(2,128)(2,1)S(1)}) fusion(bf16[2,2,2,256,256]{3,2,1,0,4:T(2,128)(2,1)S(1)} %reshape.324, s32[]{:T(128)S(6)} %select_n.119, s32[]{:T(128)S(6)} %select_n.120), kind=kLoop, calls=%fused_computation.224 | loop fusion | bytes 2097160 | tf_op jit(solution)/shard_map/jit(dynamic_index_in_dim)/dynamic_slice | solution.py:31
  162.6 9.9 %collective-permute-done.12 = bf16[2,2,256,256]{2,3,0,1:T(8,128)(2,1)S(1)} collective-permute-done((bf16[2,2,256,256]{2,3,0,1:T(8,128)(2,1)S(1)}, bf16[2,2,256,256]{2,3,0,1:T(8,128)(2,1)S(1)}, u32[]{:S(2)}, u32[]{:S(2)}) %collective-permute-start.12) | collective-permute-done | bytes 524320 | tf_op jit(solution)/shard_map/ppermute | solution.py:9
  174.7 3.4 %collective-permute-done.6 = bf16[256,256]{1,0:T(8,128)(2,1)S(1)} collective-permute-done((bf16[256,256]{1,0:T(8,128)(2,1)S(1)}, bf16[256,256]{1,0:T(8,128)(2,1)S(1)}, u32[]{:S(2)}, u32[]{:S(2)}) %collective-permute-start.6) | collective-permute-done | bytes 131104 | tf_op jit(solution)/shard_map/ppermute | solution.py:9
  182.7 2.7 %fusion.10 = bf16[256,2048]{1,0:T(8,128)(2,1)} fusion(f32[256,2048]{1,0:T(8,128)S(1)} %fusion.5, bf16[256,256]{1,0:T(8,128)(2,1)S(1)} %collective-permute-done.6, bf16[256,2048]{1,0:T(8,128)(2,1)} %collective-permute-done.11), kind=kOutput, calls=%fused_computation.16 | convolution fusion | flops 269484032 | bytes 4325376 | tf_op jit(solution)/shard_map/dot_general | solution.py:273
  186.8 3.4 %collective-permute-done.18 = bf16[2,2,32,1024]{3,2,0,1:T(8,128)(2,1)S(1)} collective-permute-done((bf16[2,2,32,1024]{3,2,0,1:T(8,128)(2,1)S(1)}, bf16[2,2,32,1024]{3,2,0,1:T(8,128)(2,1)S(1)}, u32[]{:S(2)}, u32[]{:S(2)}) %collective-permute-start.18) | collective-permute-done | bytes 262176 | tf_op jit(solution)/shard_map/ppermute | solution.py:9
  190.6 5.5 %collective-permute-done.13 = bf16[2,256,256]{1,2,0:T(8,128)(2,1)S(1)} collective-permute-done((bf16[2,256,256]{1,2,0:T(8,128)(2,1)S(1)}, bf16[2,256,256]{1,2,0:T(8,128)(2,1)S(1)}, u32[]{:S(2)}, u32[]{:S(2)}) %collective-permute-start.13) | collective-permute-done | bytes 262176 | tf_op jit(solution)/shard_map/ppermute | solution.py:9
  197.9 6.5 %collective-permute-done.14 = bf16[256,256]{0,1:T(8,128)(2,1)S(1)} collective-permute-done((bf16[256,256]{0,1:T(8,128)(2,1)S(1)}, bf16[256,256]{0,1:T(8,128)(2,1)S(1)}, u32[]{:S(2)}, u32[]{:S(2)}) %collective-permute-start.14) | collective-permute-done | bytes 131104 | tf_op jit(solution)/shard_map/ppermute | solution.py:9
  (189 shorter events, 74.9 us)
Async XLA Ops:
  0.6 26.5 %collective-permute-start.1 = (bf16[256,2048]{1,0:T(8,128)(2,1)}, bf16[256,2048]{1,0:T(8,128)(2,1)}, u32[]{:S(2)}, u32[]{:S(2)}) collective-permute-start(bf16[256,2048]{1,0:T(8,128)(2,1)} %param.25), channel_id=1, source_target_pairs={{0,2},{1,3},{2,0},{3,1},{4,6},{5,7},{6,4},{7,5},{8,10},{9,11},{10,... | collective-permute-start | bytes 3145736 | tf_op jit(solution)/shard_map/ppermute | solution.py:9
  3.7 33.0 %collective-permute-start = (bf16[256,2048]{1,0:T(8,128)(2,1)}, bf16[256,2048]{1,0:T(8,128)(2,1)}, u32[]{:S(2)}, u32[]{:S(2)}) collective-permute-start(bf16[256,2048]{1,0:T(8,128)(2,1)} %param.25), channel_id=1, source_target_pairs={{0,1},{1,0},{2,3},{3,2},{4,5},{5,4},{6,7},{7,6},{8,9},{9,8},{10,11... | collective-permute-start | bytes 3145736 | tf_op jit(solution)/shard_map/ppermute | solution.py:9
  27.2 11.2 %collective-permute-start.2 = (bf16[256,2048]{1,0:T(8,128)(2,1)}, bf16[256,2048]{1,0:T(8,128)(2,1)}, u32[]{:S(2)}, u32[]{:S(2)}) collective-permute-start(bf16[256,2048]{1,0:T(8,128)(2,1)} %collective-permute-done.1), channel_id=1, source_target_pairs={{0,1},{1,0},{2,3},{3,2},{4,5},{5,4},{6,7},{7,6},{8,9},{9,8},{10,11... | collective-permute-start | bytes 3145736 | tf_op jit(solution)/shard_map/ppermute | solution.py:9
  42.2 28.1 %all-to-all-start = ((bf16[32,48,256]{2,1,0:T(8,128)(2,1)}), bf16[32,48,256]{2,1,0:T(8,128)(2,1)}, u32[]{:S(2)}, u32[]{:S(2)}) async-start(bf16[32,48,256]{2,1,0:T(8,128)(2,1)} %bitcast.217), calls=%async_computation | async-start | bytes 1572864 | tf_op jit(solution)/shard_map/all_to_all | solution.py:206
  82.4 13.9 %collective-permute-start.22 = (bf16[2,2,2,32,1024]{4,3,0,1,2:T(8,128)(2,1)}, bf16[2,2,2,32,1024]{4,3,0,1,2:T(8,128)(2,1)}, u32[]{:S(2)}, u32[]{:S(2)}) collective-permute-start(bf16[2,2,2,32,1024]{4,3,0,1,2:T(8,128)(2,1)} %dynamic-slice_bitcast_fusion), channel_id=1, source_target_pairs={{0,2},{1,3},{2,0},{3,1},{4,6},{5,7},{6,4},{7,5},{8,10},{9,11},{10,... | collective-permute-start | bytes 1572872 | tf_op jit(solution)/shard_map/ppermute | solution.py:9
  85.1 47.4 %collective-permute-start.3 = (bf16[2,2,2,2,64,1024]{5,4,2,3,0,1:T(8,128)(2,1)}, bf16[2,2,2,2,64,1024]{5,4,2,3,0,1:T(8,128)(2,1)}, u32[]{:S(2)}, u32[]{:S(2)}) collective-permute-start(bf16[2,2,2,2,64,1024]{5,4,2,3,0,1:T(8,128)(2,1)} %bitcast.205), channel_id=1, source_target_pairs={{0,1},{1,0},{2,3},{3,2},{4,5},{5,4},{6,7},{7,6},{8,9},{9,8},{10,11... | collective-permute-start | bytes 6291464 | tf_op jit(solution)/shard_map/ppermute | solution.py:9
  99.7 32.0 %collective-permute-start.10 = (bf16[256,2048]{1,0:T(8,128)(2,1)S(1)}, bf16[256,2048]{1,0:T(8,128)(2,1)}, u32[]{:S(2)}, u32[]{:S(2)}) collective-permute-start(bf16[256,2048]{1,0:T(8,128)(2,1)S(1)} %copy-done.2), channel_id=1, source_target_pairs={{0,2},{1,3},{2,0},{3,1},{4,6},{5,7},{6,4},{7,5},{8,10},{9,11},{10,... | collective-permute-start | bytes 3145736 | tf_op jit(solution)/shard_map/ppermute | solution.py:9
  100.3 36.1 %all-to-all-start.1 = ((bf16[32,48,256]{2,1,0:T(8,128)(2,1)}), bf16[32,48,256]{2,1,0:T(8,128)(2,1)}, u32[]{:S(2)}, u32[]{:S(2)}) async-start(bf16[32,48,256]{2,1,0:T(8,128)(2,1)} %bitcast.210), calls=%async_computation.1 | async-start | bytes 1572864 | tf_op jit(solution)/shard_map/all_to_all | solution.py:206
  106.9 12.7 %collective-permute-start.24 = (bf16[2,32,1024]{2,1,0:T(8,128)(2,1)S(1)}, bf16[2,32,1024]{2,1,0:T(8,128)(2,1)}, u32[]{:S(2)}, u32[]{:S(2)}) collective-permute-start(bf16[2,32,1024]{2,1,0:T(8,128)(2,1)S(1)} %dynamic-slice_bitcast_fusion.7), channel_id=1, source_target_pairs={{0,8},{4,12},{8,0},{12,4},{16,24},{20,28},{24,16},{28,20},{1,9},{5... | collective-permute-start | bytes 393224 | tf_op jit(solution)/shard_map/ppermute | solution.py:9
  120.5 11.2 %collective-permute-start.25 = (bf16[32,1024]{1,0:T(8,128)(2,1)S(1)}, bf16[32,1024]{1,0:T(8,128)(2,1)S(1)}, u32[]{:S(2)}, u32[]{:S(2)}) collective-permute-start(bf16[32,1024]{1,0:T(8,128)(2,1)S(1)} %dynamic-slice_bitcast_fusion.11), channel_id=1, source_target_pairs={{0,16},{4,20},{8,24},{12,28},{16,0},{20,4},{24,8},{28,12},{1,17},{... | collective-permute-start | bytes 196616 | tf_op jit(solution)/shard_map/ppermute | solution.py:9
  125.3 55.2 %collective-permute-start.9 = (bf16[256,2048]{1,0:T(8,128)(2,1)S(1)}, bf16[256,2048]{1,0:T(8,128)(2,1)}, u32[]{:S(2)}, u32[]{:S(2)}) collective-permute-start(bf16[256,2048]{1,0:T(8,128)(2,1)S(1)} %copy-done.2), channel_id=1, source_target_pairs={{0,1},{1,0},{2,3},{3,2},{4,5},{5,4},{6,7},{7,6},{8,9},{9,8},{10,11... | collective-permute-start | bytes 3145736 | tf_op jit(solution)/shard_map/ppermute | solution.py:9
  131.8 51.0 %collective-permute-start.11 = (bf16[256,2048]{1,0:T(8,128)(2,1)}, bf16[256,2048]{1,0:T(8,128)(2,1)}, u32[]{:S(2)}, u32[]{:S(2)}) collective-permute-start(bf16[256,2048]{1,0:T(8,128)(2,1)} %collective-permute-done.10), channel_id=1, source_target_pairs={{0,1},{1,0},{2,3},{3,2},{4,5},{5,4},{6,7},{7,6},{8,9},{9,8},{10,11... | collective-permute-start | bytes 3145736 | tf_op jit(solution)/shard_map/ppermute | solution.py:9
  143.0 15.1 %collective-permute-start.7 = (bf16[2,2,2,32,1024]{4,3,2,0,1:T(8,128)(2,1)}, bf16[2,2,2,32,1024]{4,3,2,0,1:T(8,128)(2,1)}, u32[]{:S(2)}, u32[]{:S(2)}) collective-permute-start(bf16[2,2,2,32,1024]{4,3,2,0,1:T(8,128)(2,1)} %dynamic-slice_bitcast_fusion.2), channel_id=1, source_target_pairs={{0,4},{4,0},{8,12},{12,8},{16,20},{20,16},{24,28},{28,24},{1,5},{5... | collective-permute-start | bytes 1572872 | tf_op jit(solution)/shard_map/ppermute | solution.py:9
  144.5 15.4 %collective-permute-start.8 = (bf16[2,2,2,32,1024]{4,3,1,2,0:T(8,128)(2,1)}, bf16[2,2,2,32,1024]{4,3,1,2,0:T(8,128)(2,1)}, u32[]{:S(2)}, u32[]{:S(2)}) collective-permute-start(bf16[2,2,2,32,1024]{4,3,1,2,0:T(8,128)(2,1)} %dynamic-slice_bitcast_fusion.1), channel_id=1, source_target_pairs={{0,8},{4,12},{8,0},{12,4},{16,24},{20,28},{24,16},{28,20},{1,9},{5... | collective-permute-start | bytes 1572872 | tf_op jit(solution)/shard_map/ppermute | solution.py:9
  146.1 26.7 %collective-permute-start.4 = (bf16[256,256]{1,0:T(8,128)(2,1)}, bf16[256,256]{1,0:T(8,128)(2,1)S(1)}, u32[]{:S(2)}, u32[]{:S(2)}) collective-permute-start(bf16[256,256]{1,0:T(8,128)(2,1)} %fusion.29), channel_id=1, source_target_pairs={{0,1},{1,0},{2,3},{3,2},{4,5},{5,4},{6,7},{7,6},{8,9},{9,8},{10,11... | collective-permute-start | bytes 393224 | tf_op jit(solution)/shard_map/ppermute | solution.py:9
  158.1 14.4 %collective-permute-start.12 = (bf16[2,2,256,256]{2,3,0,1:T(8,128)(2,1)S(1)}, bf16[2,2,256,256]{2,3,0,1:T(8,128)(2,1)S(1)}, u32[]{:S(2)}, u32[]{:S(2)}) collective-permute-start(bf16[2,2,256,256]{2,3,0,1:T(8,128)(2,1)S(1)} %bitcast.218), channel_id=1, source_target_pairs={{0,4},{4,0},{8,12},{12,8},{16,20},{20,16},{24,28},{28,24},{1,5},{5... | collective-permute-start | bytes 1572872 | tf_op jit(solution)/shard_map/ppermute | solution.py:9
  159.9 14.8 %collective-permute-start.5 = (bf16[256,256]{1,0:T(8,128)(2,1)S(1)}, bf16[256,256]{1,0:T(8,128)(2,1)S(1)}, u32[]{:S(2)}, u32[]{:S(2)}) collective-permute-start(bf16[256,256]{1,0:T(8,128)(2,1)S(1)} %copy-done.17), channel_id=1, source_target_pairs={{0,2},{1,3},{2,0},{3,1},{4,6},{5,7},{6,4},{7,5},{8,10},{9,11},{10,... | collective-permute-start | bytes 393224 | tf_op jit(solution)/shard_map/ppermute | solution.py:9
  172.9 13.6 %collective-permute-start.15 = (bf16[2,2,32,1024]{3,2,1,0:T(8,128)(2,1)S(1)}, bf16[2,2,32,1024]{3,2,1,0:T(8,128)(2,1)S(1)}, u32[]{:S(2)}, u32[]{:S(2)}) collective-permute-start(bf16[2,2,32,1024]{3,2,1,0:T(8,128)(2,1)S(1)} %dynamic-slice_bitcast_fusion.5), channel_id=1, source_target_pairs={{0,8},{4,12},{8,0},{12,4},{16,24},{20,28},{24,16},{28,20},{1,9},{5... | collective-permute-start | bytes 786440 | tf_op jit(solution)/shard_map/ppermute | solution.py:9
  174.7 15.5 %collective-permute-start.18 = (bf16[2,2,32,1024]{3,2,0,1:T(8,128)(2,1)S(1)}, bf16[2,2,32,1024]{3,2,0,1:T(8,128)(2,1)S(1)}, u32[]{:S(2)}, u32[]{:S(2)}) collective-permute-start(bf16[2,2,32,1024]{3,2,0,1:T(8,128)(2,1)S(1)} %dynamic-slice_bitcast_fusion.4), channel_id=1, source_target_pairs={{0,16},{4,20},{8,24},{12,28},{16,0},{20,4},{24,8},{28,12},{1,17},{... | collective-permute-start | bytes 786440 | tf_op jit(solution)/shard_map/ppermute | solution.py:9
  178.1 18.0 %collective-permute-start.13 = (bf16[2,256,256]{1,2,0:T(8,128)(2,1)S(1)}, bf16[2,256,256]{1,2,0:T(8,128)(2,1)S(1)}, u32[]{:S(2)}, u32[]{:S(2)}) collective-permute-start(bf16[2,256,256]{1,2,0:T(8,128)(2,1)S(1)} %dynamic-slice_bitcast_fusion.6), channel_id=1, source_target_pairs={{0,8},{4,12},{8,0},{12,4},{16,24},{20,28},{24,16},{28,20},{1,9},{5... | collective-permute-start | bytes 786440 | tf_op jit(solution)/shard_map/ppermute | solution.py:9
  186.5 9.8 %collective-permute-start.16 = (bf16[2,32,1024]{2,1,0:T(8,128)(2,1)S(1)}, bf16[2,32,1024]{2,1,0:T(8,128)(2,1)S(1)}, u32[]{:S(2)}, u32[]{:S(2)}) collective-permute-start(bf16[2,32,1024]{2,1,0:T(8,128)(2,1)S(1)} %dynamic-slice_bitcast_fusion.9), channel_id=1, source_target_pairs={{0,16},{4,20},{8,24},{12,28},{16,0},{20,4},{24,8},{28,12},{1,17},{... | collective-permute-start | bytes 393224 | tf_op jit(solution)/shard_map/ppermute | solution.py:9
  196.2 8.2 %collective-permute-start.14 = (bf16[256,256]{0,1:T(8,128)(2,1)S(1)}, bf16[256,256]{0,1:T(8,128)(2,1)S(1)}, u32[]{:S(2)}, u32[]{:S(2)}) collective-permute-start(bf16[256,256]{0,1:T(8,128)(2,1)S(1)} %dynamic-slice_bitcast_fusion.10), channel_id=1, source_target_pairs={{0,16},{4,20},{8,24},{12,28},{16,0},{20,4},{24,8},{28,12},{1,17},{... | collective-permute-start | bytes 393224 | tf_op jit(solution)/shard_map/ppermute | solution.py:9
  196.4 8.8 %collective-permute-start.17 = (bf16[32,1024]{1,0:T(8,128)(2,1)S(1)}, bf16[32,1024]{1,0:T(8,128)(2,1)S(1)}, u32[]{:S(2)}, u32[]{:S(2)}) collective-permute-start(bf16[32,1024]{1,0:T(8,128)(2,1)S(1)} %dynamic-slice_bitcast_fusion.13), channel_id=1, source_target_pairs={{0,2},{1,3},{2,0},{3,1},{4,6},{5,7},{6,4},{7,5},{8,10},{9,11},{10,... | collective-permute-start | bytes 196616 | tf_op jit(solution)/shard_map/ppermute | solution.py:9
  197.7 7.5 %collective-permute-start.20 = (bf16[32,1024]{1,0:T(8,128)(2,1)S(1)}, bf16[32,1024]{1,0:T(8,128)(2,1)S(1)}, u32[]{:S(2)}, u32[]{:S(2)}) collective-permute-start(bf16[32,1024]{1,0:T(8,128)(2,1)S(1)} %dynamic-slice_bitcast_fusion.12), channel_id=1, source_target_pairs={{0,4},{4,0},{8,12},{12,8},{16,20},{20,16},{24,28},{28,24},{1,5},{5... | collective-permute-start | bytes 196616 | tf_op jit(solution)/shard_map/ppermute | solution.py:9
  (28 other events, 174.3 us)
where the time goes:
time: 207 us; the launch traced here: 206 us
  waiting for transfers between devices  82.5 us (40%)
  matrix products  45.4 us (22%)
  starting transfers between devices  30.3 us (15%)
  other arithmetic  28.7 us (14%)
  local copies, waits for them, and re-layouts  17.7 us (9%)
    ppermute x26, waiting for transfers between devices, exchange(): lax.ppermute(value, axis_name, [(rank, rank ^ flip) for rank in range(siz...  65 us
    ppermute x26, starting transfers between devices, exchange(): lax.ppermute(value, axis_name, [(rank, rank ^ flip) for rank in range(siz...  20.3 us
    all_to_all x2, waiting for transfers between devices, spread(): lax.all_to_all(values.reshape(device_count, slot_count, feature_part), ('...  17.4 us
    dot_general x13, matrix products, pick(): jnp.dot(chosen, rows, preferred_element_type=jnp.float32)  11.6 us
    all_to_all x2, starting transfers between devices, spread(): lax.all_to_all(values.reshape(device_count, slot_count, feature_part), ('...  10 us
    convert_element_type x13, other arithmetic, fold_scatter(): value = value.astype(jnp.bfloat16)  9.48 us
    dot_general x6, matrix products, rows_product(): lax.dot_general(left, right, (((0,), (0,)), ((), ())), preferred_element_...  8.78 us
    add x1, other arithmetic, depthwise(): running_sum + kernel[tap_index] * padded[tap_index:tap_index + row_total]...  7.6 us
  transfers between devices with their start and end apart: 28, of which 12 were waited for; matrix products, arithmetic and copies ran while one was open for 37% of the time, Pallas kernels for 0%

commit v1 on v0

--- a/solution.py
+++ b/solution.py
@@ -21,20 +21,15 @@
     return [blocks[flip] for flip in range(lax.axis_size(axis_name))]
 
 
-def fold_scatter(value, order, dims, last=False):
-    layout = sorted(dims, key=lambda step: (step[0] != "ctx", -step[1]))
-    for position, step in enumerate(order):
-        axis_name, bit = step
-        dim = layout.index(step)
-        layout.remove(step)
-        mine = (lax.axis_index(axis_name) >> bit) & 1
-        keep = lax.dynamic_index_in_dim(value, mine, dim, keepdims=False)
-        send = lax.dynamic_index_in_dim(value, 1 - mine, dim, keepdims=False)
-        came = exchange(send, axis_name, 1 << bit)
-        value = keep.astype(jnp.float32) + came.astype(jnp.float32)
-        if not last or position + 1 < len(order):
-            value = value.astype(jnp.bfloat16)
-    return value
+def fold_step(value, dims, step, last=False):
+    axis_name, bit = step
+    dim = sorted(dims, key=lambda entry: (entry[0] != "ctx", -entry[1])).index(step)
+    mine = (lax.axis_index(axis_name) >> bit) & 1
+    keep = lax.dynamic_index_in_dim(value, mine, dim, keepdims=False)
+    send = lax.dynamic_index_in_dim(value, 1 - mine, dim, keepdims=False)
+    came = exchange(send, axis_name, 1 << bit)
+    value = keep.astype(jnp.float32) + came.astype(jnp.float32)
+    return value if last else value.astype(jnp.bfloat16)
 
 
 def split_bits(value, steps):
@@ -119,10 +114,7 @@
     _, raised, mixed_rows, _ = kept_state
     model_width = output_grad.shape[1]
     act_grad = lax.dot_general(
-        output_grad,
-        pointwise_two,
-        (((1,), (1,)), ((), ())),
-        preferred_element_type=jnp.float32,
+        output_grad, pointwise_two, (((1,), (1,)), ((), ())), preferred_element_type=jnp.float32
     )
     sigmoid_mix = jax.nn.sigmoid(mixed_rows)
     mixed_grad = act_grad * (sigmoid_mix + mixed_rows * sigmoid_mix * (1.0 - sigmoid_mix))
@@ -176,7 +168,7 @@
     slot_count = 3 * encoded_rows // (2 * ctx_count)
     ctx_steps = [("ctx", bit) for bit in range(axis_bits("ctx"))]
     tp_steps = [("tp", bit) for bit in range(axis_bits("tp"))]
-    near, far = tp_steps[:1], tp_steps[1:]
+    far = tp_steps[1:]
     step_count = len(ctx_steps) + len(tp_steps)
 
     slot_index = jnp.arange(slot_count, dtype=jnp.int32)
@@ -220,9 +212,12 @@
             for cot in cot_blocks
         ]
     )
-    parcel = pick(place_of_slot, jnp.concatenate(places), frame_back)
+    placing = lax.optimization_barrier(
+        (jnp.concatenate(places)[:, None] == place_of_slot[None, :]).astype(jnp.bfloat16)
+    )
+    parcel = rows_product(placing, frame_back).astype(jnp.bfloat16)
     returned = spread(parcel)
-    late_projector, _ = lax.optimization_barrier((projector, cot_blocks[-1]))
+    late_projector, _ = lax.optimization_barrier((projector, cot_blocks[tp_count // 2]))
     projector_blocks = gather_blocks(late_projector, "tp")
 
     inputs = subsample(mel_frames, input_proj, sub_depthwise, sub_pointwise, output_proj)
@@ -234,7 +229,9 @@
     outgoing = jnp.concatenate(
         [pick(row_of_slot, local_rows, part) for part in jnp.split(encoded, tp_count, axis=1)]
     )
-    returned, outgoing = lax.optimization_barrier((returned, outgoing))
+    returned, outgoing, projector_blocks = lax.optimization_barrier(
+        (returned, outgoing, projector_blocks)
+    )
     arrived = spread(outgoing).reshape(device_count * slot_count, feature_part)
 
     returned = returned.reshape(tp_count, ctx_count * slot_count, feature_part)
@@ -244,35 +241,46 @@
     two_grad = rows_product(output_grad, activated).astype(jnp.bfloat16)
     raised_grad = raised_backward(output_grad, segments, depthwise_taps, pointwise_two, kept_state)
     one_grad = rows_product(raised_grad, normed).astype(jnp.bfloat16)
-    one_near = fold_scatter(split_bits(one_grad, step_count), near, ctx_steps + tp_steps)
-    two_near = fold_scatter(split_bits(two_grad, step_count), near, ctx_steps + tp_steps)
+    all_steps = ctx_steps + tp_steps
+    near = tp_steps[0]
+    two_near = fold_step(split_bits(two_grad, step_count), all_steps, near)
+    one_near = fold_step(split_bits(one_grad, step_count), all_steps, near)
+    one_near, two_near = lax.optimization_barrier((one_near, two_near))
     arrived, _ = lax.optimization_barrier((arrived, one_near))
-    rest = ctx_steps + far
     half = one_near.shape[-2] // 2
     parts = [one_near[..., :half, :], one_near[..., half:, :], two_near]
     orders = [ctx_steps + far, ctx_steps[1:] + far + ctx_steps[:1], far + ctx_steps]
-    parts = [fold_scatter(part, order[:1], rest) for part, order in zip(parts, orders)]
-    after_first = parts[0], parts[1]
-    parts = [
-        fold_scatter(part, order[1:], [step for step in rest if step != order[0]], last=True)
-        for part, order in zip(parts, orders)
-    ]
-    one_part = jnp.concatenate(parts[:2], axis=0).T
-    two_part = parts[2].T
-
-    frame_blocks = [pick(place, place_of_slot, arrived) for place in places]
-    weight_sum = sum(rows_product(cot, held) for cot, held in zip(cot_blocks, frame_blocks))
-    projector_grad = fold_scatter(
-        split_bits(weight_sum.astype(jnp.bfloat16), len(ctx_steps)), ctx_steps, ctx_steps, last=True
-    ).T
+
+    def advance(parts, position):
+        return [
+            fold_step(part, order[position:], order[position], position + 1 == len(order))
+            for part, order in zip(parts, orders)
+        ]
+
+    parts = advance(parts, 0)
+    framed = jnp.dot(placing, arrived, preferred_element_type=jnp.float32)
+    framed = framed.astype(jnp.bfloat16)
+    parts = lax.optimization_barrier(parts)
+    frame_blocks = jnp.split(framed, tp_count)
     row_blocks = [frame_blocks[0]] + [
         exchange(frame_blocks[flip], "tp", flip) for flip in range(1, tp_count)
     ]
-    row_blocks, _ = lax.optimization_barrier((row_blocks, after_first))
+    weight_sum = sum(rows_product(cot, held) for cot, held in zip(cot_blocks, frame_blocks))
+    weight = split_bits(weight_sum.astype(jnp.bfloat16), len(ctx_steps))
+    row_blocks, _ = lax.optimization_barrier((row_blocks, parts))
     llm_embed = sum(
         jnp.dot(held, weights, preferred_element_type=jnp.float32)
         for held, weights in zip(row_blocks, projector_blocks)
     ).astype(jnp.bfloat16)
+    left = len(orders[0]) - len(ctx_steps) + 1
+    for position in range(1, left):
+        parts = lax.optimization_barrier(advance(parts, position))
+    for taken, position in enumerate(range(left, len(orders[0]))):
+        weight = fold_step(weight, ctx_steps[taken:], ctx_steps[taken])
+        parts, weight = lax.optimization_barrier((advance(parts, position), weight))
+    projector_grad = fold_step(weight, ctx_steps[-1:], ctx_steps[-1], last=True).T
+    one_part = jnp.concatenate(parts[:2], axis=0).T
+    two_part = parts[2].T
     return (llm_embed, projector_grad, one_part, two_part)
 
 

time: 207 us -> 181 us (0.87)
  waiting for transfers between devices: 82.5 us -> 67.5 us
  matrix products: 45.4 us -> 36.1 us
  other arithmetic: 28.7 us -> 19.6 us
  starting transfers between devices: 30.3 us -> 35.5 us
    ppermute x26, waiting for transfers between devices: 65 us -> 53.1 us  [exchange(): lax.ppermute(value, axis_name, [(rank, rank ^ flip) for rank in range(siz...]
    dot_general x13 -> x8, matrix products: 11.6 us -> 2.18 us  [pick(): jnp.dot(chosen, rows, preferred_element_type=jnp.float32)]
    add x1, other arithmetic: 7.6 us -> 2.62 us  [depthwise(): running_sum + kernel[tap_index] * padded[tap_index:tap_index + row_total]...]
    ppermute x26, starting transfers between devices: 20.3 us -> 23.6 us  [exchange(): lax.ppermute(value, axis_name, [(rank, rank ^ flip) for rank in range(siz...]
    dot_general x0 -> x1, matrix products: none -> 3.14 us  [body(): framed = jnp.dot(placing, arrived, preferred_element_type=jnp.float32)]
    all_to_all x2, waiting for transfers between devices: 17.4 us -> 14.4 us  [spread(): lax.all_to_all(values.reshape(device_count, slot_count, feature_part), ('...]
    mul x1, other arithmetic: 2.95 us -> 0.28 us  [conv_forward(): raised[:, :model_width] * jax.nn.sigmoid(raised[:, model_width:])]
    unnamed x48 -> x50, local copies, waits for them, and re-layouts: 3.9 us -> 4.89 us
  transfers between devices with their start and end apart: 28 -> 28, of which waited for: 12 -> 14; matrix products, arithmetic and copies ran while one was open for 37% -> 28% of each run, Pallas kernels for 0% -> 0%
where the time goes in v1:
time: 181 us; the launch traced here: 180 us
  waiting for transfers between devices  67.5 us (37%)
  matrix products  36.1 us (20%)
  starting transfers between devices  35.5 us (20%)
  local copies, waits for them, and re-layouts  19.6 us (11%)
  other arithmetic  19.6 us (11%)
    ppermute x26, waiting for transfers between devices, exchange(): lax.ppermute(value, axis_name, [(rank, rank ^ flip) for rank in range(siz...  53.1 us
    ppermute x26, starting transfers between devices, exchange(): lax.ppermute(value, axis_name, [(rank, rank ^ flip) for rank in range(siz...  23.6 us
    all_to_all x2, waiting for transfers between devices, spread(): lax.all_to_all(values.reshape(device_count, slot_count, feature_part), ('...  14.4 us
    all_to_all x2, starting transfers between devices, spread(): lax.all_to_all(values.reshape(device_count, slot_count, feature_part), ('...  12 us
    dot_general x7, matrix products, rows_product(): lax.dot_general(left, right, (((0,), (0,)), ((), ())), preferred_element_...  9.54 us
    convert_element_type x13, other arithmetic, fold_step(): return value if last else value.astype(jnp.bfloat16)  6.83 us
    dot_general x4, matrix products, body(): jnp.dot(held, weights, preferred_element_type=jnp.float32)  5.27 us
    unnamed x50, local copies, waits for them, and re-layouts  4.89 us
  transfers between devices with their start and end apart: 28, of which 14 were waited for; matrix products, arithmetic and copies ran while one was open for 28% of the time, Pallas kernels for 0%

profile of v1, /device:TPU:0, one launch (start us, length us, event | category | flops | bytes accessed | tf_op | source)
XLA Modules:
  0.0 179.9 jit_solution(7987866291674293987)
XLA Ops:
  0.6 3.1 %collective-permute-start.1 = (bf16[256,2048]{1,0:T(8,128)(2,1)}, bf16[256,2048]{1,0:T(8,128)(2,1)}, u32[]{:S(2)}, u32[]{:S(2)}) collective-permute-start(bf16[256,2048]{1,0:T(8,128)(2,1)} %param.25), channel_id=1, source_target_pairs={{0,2},{1,3},{2,0},{3,1},{4,6},{5,7},{6,4},{7,5},{8,10},{9,11},{10,... | collective-permute-start | bytes 3145736 | tf_op jit(solution)/shard_map/ppermute | solution.py:9
  12.9 2.2 %compare_convert_fusion = bf16[1024,1536]{1,0:T(8,128)(2,1)} fusion(s32[1536]{0:T(1024)S(1)} %select_n.112, s32[1024]{0:T(1024)S(1)} %pad_add_fusion), kind=kLoop, calls=%fused_computation | loop fusion | flops 3145728 | bytes 3155968 | tf_op jit(solution)/shard_map/convert_element_type | solution.py:216
  15.6 3.5 %fusion.111 = f32[256,2048]{1,0:T(8,128)S(1)} fusion(bf16[1024,2048]{1,0:T(8,128)(2,1)} %param.21, f32[256,1024]{1,0:T(8,128)S(1)} %get-tuple-element.117, f32[1024]{0:T(1024)S(1)} %convert_element_type.423, f32[256]{0:T(256)S(1)} %add_rsqrt_fusion, f32[256]{0:T(256)S(1)} %broadcast_multiply_fusion.8), kind=kOutput, calls=%fused_computation.249 | convolution fusion | flops 1074790400 | bytes 7346176 | tf_op jit(solution)/shard_map/dot_general | solution.py:102
  22.0 5.2 %collective-permute-done.1 = bf16[256,2048]{1,0:T(8,128)(2,1)} collective-permute-done((bf16[256,2048]{1,0:T(8,128)(2,1)}, bf16[256,2048]{1,0:T(8,128)(2,1)}, u32[]{:S(2)}, u32[]{:S(2)}) %collective-permute-start.1) | collective-permute-done | bytes 1048608 | tf_op jit(solution)/shard_map/ppermute | solution.py:9
  27.3 2.6 %multiply_add_fusion = f32[256,1024]{1,0:T(8,128)} fusion(f32[256,1024]{1,0:T(8,128)S(1)} %slice_multiply_fusion.2, f32[256]{0:T(256)S(1)} %get-tuple-element.115, f32[1024]{0:T(1024)S(1)} %bitcast.234, f32[256]{0:T(256)S(1)} %get-tuple-element.109, f32[1024]{0:T(1024)S(1)} %bitcast.232, f32[256]{0:T(256)S(1)} %get-tuple-element.110, f32[1024]{0:T(1024)S(1)} %bitcast.230, ...), kind=kLoop, calls=%fused_computation.92 | loop fusion | flops 6553600 | bytes 2142208 | tf_op jit(solution)/shard_map/add | solution.py:76
  35.7 2.0 %convolution_convert_fusion.1 = bf16[1536,256]{1,0:T(8,128)(2,1)} fusion(bf16[1024,1536]{1,0:T(8,128)(2,1)S(1)} %copy-done.16, bf16[256,256]{1,0:T(8,128)(2,1)S(1)} %convolution_convert_fusion.12, bf16[256,256]{1,0:T(8,128)(2,1)S(1)} %convolution_convert_fusion.13, bf16[256,256]{1,0:T(8,128)(2,1)S(1)} %convolution_convert_fusion.14, ...), kind=kOutput, calls=%fused_computation.13 | convolution fusion | flops 807796736 | bytes 4456448 | tf_op jit(solution)/shard_map/dot_general | solution.py:133
  37.7 5.2 %all-to-all-start = ((bf16[32,48,256]{2,1,0:T(8,128)(2,1)}), bf16[32,48,256]{2,1,0:T(8,128)(2,1)}, u32[]{:S(2)}, u32[]{:S(2)}) async-start(bf16[32,48,256]{2,1,0:T(8,128)(2,1)} %bitcast.210), calls=%async_computation | async-start | bytes 1572864 | tf_op jit(solution)/shard_map/all_to_all | solution.py:198
  42.9 2.3 %fusion.8 = bf16[256,1024]{1,0:T(8,128)(2,1)S(1)} fusion(f32[256,1024]{1,0:T(8,128)} %copy-done.9, bf16[1024,1024]{1,0:T(8,128)(2,1)S(1)} %copy-done, f32[256,1024]{1,0:T(8,128)} %multiply_add_fusion), kind=kOutput, calls=%fused_computation.24 | convolution fusion | flops 538705920 | bytes 4718592 | tf_op jit(solution)/shard_map/dot_general | solution.py:108
  45.2 17.9 %collective-permute-done.4 = bf16[256,2048]{1,0:T(8,128)(2,1)} collective-permute-done((bf16[256,2048]{1,0:T(8,128)(2,1)S(1)}, bf16[256,2048]{1,0:T(8,128)(2,1)}, u32[]{:S(2)}, u32[]{:S(2)}) %collective-permute-start.4) | collective-permute-done | bytes 1048608 | tf_op jit(solution)/shard_map/ppermute | solution.py:9
  80.1 6.8 %all-to-all-start.1 = ((bf16[32,48,256]{2,1,0:T(8,128)(2,1)}), bf16[32,48,256]{2,1,0:T(8,128)(2,1)}, u32[]{:S(2)}, u32[]{:S(2)}) async-start(bf16[32,48,256]{2,1,0:T(8,128)(2,1)} %bitcast.204), calls=%async_computation.1 | async-start | bytes 1572864 | tf_op jit(solution)/shard_map/all_to_all | solution.py:198
  86.9 2.9 %fusion.7 = bf16[2,2,2,2,32,1024]{5,4,0,1,2,3:T(8,128)(2,1)} fusion(bf16[2,2,2,2,32,1024]{5,4,0,1,2,3:T(8,128)(2,1)} %collective-permute-done.7, bf16[2,2,2,2,1,32,1024]{6,5,4,3,2,1,0:T(8,128)(2,1)} %get-tuple-element.68), kind=kLoop, calls=%fused_computation.18 | loop fusion | flops 2097152 | bytes 3145728 | tf_op jit(solution)/shard_map/convert_element_type | solution.py:32
  89.9 2.7 %fusion = bf16[2,2,2,2,64,1024]{5,4,2,3,0,1:T(8,128)(2,1)S(1)} fusion(bf16[2,2,2,2,64,1024]{5,4,2,3,0,1:T(8,128)(2,1)} %collective-permute-done.6, bf16[2,2,2,2,1,64,1024]{6,5,4,3,2,1,0:T(8,128)(2,1)S(1)} %get-tuple-element.64), kind=kLoop, calls=%fused_computation.2 | loop fusion | flops 4194304 | bytes 6291456 | tf_op jit(solution)/shard_map/convert_element_type | solution.py:32
  94.1 14.4 %all-to-all-done.1 = bf16[32,48,256]{2,1,0:T(8,128)(2,1)} async-done(((bf16[32,48,256]{2,1,0:T(8,128)(2,1)}), bf16[32,48,256]{2,1,0:T(8,128)(2,1)}, u32[]{:S(2)}, u32[]{:S(2)}) %all-to-all-start.1) | async-done | bytes 786464 | tf_op jit(solution)/shard_map/all_to_all | solution.py:198
  108.5 3.1 %convolution_convert_fusion.3 = bf16[1024,256]{1,0:T(8,128)(2,1)S(1)} fusion(bf16[1024,1536]{1,0:T(8,128)(2,1)} %compare_convert_fusion, bf16[1536,256]{1,0:T(8,128)(2,1)} %bitcast.36), kind=kOutput, calls=%fused_computation.26 | convolution fusion | flops 805568512 | bytes 4456448 | tf_op jit(solution)/shard_map/dot_general | solution.py:261
  122.2 2.2 %constant_dynamic-slice_fusion.1 = (bf16[2,2,1,256,256]{3,2,1,0,4:T(2,128)(2,1)S(1)}, bf16[2,2,1,256,256]{3,2,1,0,4:T(2,128)(2,1)S(1)}) fusion(bf16[2,2,2,256,256]{3,2,1,0,4:T(2,128)(2,1)S(1)} %reshape.308, s32[]{:T(128)S(6)} %select_n.119, s32[]{:T(128)S(6)} %select_n.120), kind=kLoop, calls=%fused_computation.199 | loop fusion | bytes 2097160 | tf_op jit(solution)/shard_map/jit(dynamic_index_in_dim)/dynamic_slice | solution.py:28
  126.2 9.5 %collective-permute-done.11 = bf16[2,2,2,32,1024]{4,3,2,0,1:T(8,128)(2,1)S(1)} collective-permute-done((bf16[2,2,2,32,1024]{4,3,2,0,1:T(8,128)(2,1)S(1)}, bf16[2,2,2,32,1024]{4,3,2,0,1:T(8,128)(2,1)S(1)}, u32[]{:S(2)}, u32[]{:S(2)}) %collective-permute-start.11) | collective-permute-done | bytes 524320 | tf_op jit(solution)/shard_map/ppermute | solution.py:9
  139.0 2.0 %collective-permute-start.14 = (bf16[2,2,32,1024]{3,2,1,0:T(8,128)(2,1)S(1)}, bf16[2,2,32,1024]{3,2,1,0:T(8,128)(2,1)S(1)}, u32[]{:S(2)}, u32[]{:S(2)}) collective-permute-start(bf16[2,2,32,1024]{3,2,1,0:T(8,128)(2,1)S(1)} %dynamic-slice_bitcast_fusion.6), channel_id=1, source_target_pairs={{0,8},{4,12},{8,0},{12,4},{16,24},{20,28},{24,16},{28,20},{1,9},{5... | collective-permute-start | bytes 786440 | tf_op jit(solution)/shard_map/ppermute | solution.py:9
  147.1 4.6 %collective-permute-done.16 = bf16[2,2,32,1024]{3,2,0,1:T(8,128)(2,1)S(1)} collective-permute-done((bf16[2,2,32,1024]{3,2,0,1:T(8,128)(2,1)S(1)}, bf16[2,2,32,1024]{3,2,0,1:T(8,128)(2,1)S(1)}, u32[]{:S(2)}, u32[]{:S(2)}) %collective-permute-start.16) | collective-permute-done | bytes 262176 | tf_op jit(solution)/shard_map/ppermute | solution.py:9
  154.5 2.0 %collective-permute-start.17 = (bf16[2,32,1024]{2,1,0:T(8,128)(2,1)S(1)}, bf16[2,32,1024]{2,1,0:T(8,128)(2,1)S(1)}, u32[]{:S(2)}, u32[]{:S(2)}) collective-permute-start(bf16[2,32,1024]{2,1,0:T(8,128)(2,1)S(1)} %dynamic-slice_bitcast_fusion.10), channel_id=1, source_target_pairs={{0,16},{4,20},{8,24},{12,28},{16,0},{20,4},{24,8},{28,12},{1,17},{... | collective-permute-start | bytes 393224 | tf_op jit(solution)/shard_map/ppermute | solution.py:9
  156.5 3.4 %collective-permute-done.19 = bf16[2,32,1024]{2,1,0:T(8,128)(2,1)S(1)} collective-permute-done((bf16[2,32,1024]{2,1,0:T(8,128)(2,1)S(1)}, bf16[2,32,1024]{2,1,0:T(8,128)(2,1)S(1)}, u32[]{:S(2)}, u32[]{:S(2)}) %collective-permute-start.19) | collective-permute-done | bytes 131104 | tf_op jit(solution)/shard_map/ppermute | solution.py:9
  160.1 3.1 %collective-permute-done.17 = bf16[2,32,1024]{2,1,0:T(8,128)(2,1)S(1)} collective-permute-done((bf16[2,32,1024]{2,1,0:T(8,128)(2,1)S(1)}, bf16[2,32,1024]{2,1,0:T(8,128)(2,1)S(1)}, u32[]{:S(2)}, u32[]{:S(2)}) %collective-permute-start.17) | collective-permute-done | bytes 131104 | tf_op jit(solution)/shard_map/ppermute | solution.py:9
  163.4 2.1 %collective-permute-start.23 = (bf16[32,1024]{1,0:T(8,128)(2,1)S(1)}, bf16[32,1024]{1,0:T(8,128)(2,1)S(1)}, u32[]{:S(2)}, u32[]{:S(2)}) collective-permute-start(bf16[32,1024]{1,0:T(8,128)(2,1)S(1)} %dynamic-slice_bitcast_fusion.11), channel_id=1, source_target_pairs={{0,16},{4,20},{8,24},{12,28},{16,0},{20,4},{24,8},{28,12},{1,17},{... | collective-permute-start | bytes 196616 | tf_op jit(solution)/shard_map/ppermute | solution.py:9
  171.9 2.0 %collective-permute-start.25 = (bf16[256,256]{0,1:T(8,128)(2,1)S(1)}, bf16[256,256]{0,1:T(8,128)(2,1)S(1)}, u32[]{:S(2)}, u32[]{:S(2)}) collective-permute-start(bf16[256,256]{0,1:T(8,128)(2,1)S(1)} %dynamic-slice_bitcast_fusion.7), channel_id=1, source_target_pairs={{0,16},{4,20},{8,24},{12,28},{16,0},{20,4},{24,8},{28,12},{1,17},{... | collective-permute-start | bytes 393224 | tf_op jit(solution)/shard_map/ppermute | solution.py:9
  176.1 3.0 %collective-permute-done.25 = bf16[256,256]{0,1:T(8,128)(2,1)S(1)} collective-permute-done((bf16[256,256]{0,1:T(8,128)(2,1)S(1)}, bf16[256,256]{0,1:T(8,128)(2,1)S(1)}, u32[]{:S(2)}, u32[]{:S(2)}) %collective-permute-start.25) | collective-permute-done | bytes 131104 | tf_op jit(solution)/shard_map/ppermute | solution.py:9
  (190 shorter events, 70.6 us)
Async XLA Ops:
  0.6 26.5 %collective-permute-start.1 = (bf16[256,2048]{1,0:T(8,128)(2,1)}, bf16[256,2048]{1,0:T(8,128)(2,1)}, u32[]{:S(2)}, u32[]{:S(2)}) collective-permute-start(bf16[256,2048]{1,0:T(8,128)(2,1)} %param.25), channel_id=1, source_target_pairs={{0,2},{1,3},{2,0},{3,1},{4,6},{5,7},{6,4},{7,5},{8,10},{9,11},{10,... | collective-permute-start | bytes 3145736 | tf_op jit(solution)/shard_map/ppermute | solution.py:9
  3.7 29.6 %collective-permute-start = (bf16[256,2048]{1,0:T(8,128)(2,1)}, bf16[256,2048]{1,0:T(8,128)(2,1)}, u32[]{:S(2)}, u32[]{:S(2)}) collective-permute-start(bf16[256,2048]{1,0:T(8,128)(2,1)} %param.25), channel_id=1, source_target_pairs={{0,1},{1,0},{2,3},{3,2},{4,5},{5,4},{6,7},{7,6},{8,9},{9,8},{10,11... | collective-permute-start | bytes 3145736 | tf_op jit(solution)/shard_map/ppermute | solution.py:9
  27.2 8.0 %collective-permute-start.2 = (bf16[256,2048]{1,0:T(8,128)(2,1)}, bf16[256,2048]{1,0:T(8,128)(2,1)S(1)}, u32[]{:S(2)}, u32[]{:S(2)}) collective-permute-start(bf16[256,2048]{1,0:T(8,128)(2,1)} %collective-permute-done.1), channel_id=1, source_target_pairs={{0,1},{1,0},{2,3},{3,2},{4,5},{5,4},{6,7},{7,6},{8,9},{9,8},{10,11... | collective-permute-start | bytes 3145736 | tf_op jit(solution)/shard_map/ppermute | solution.py:9
  29.9 33.2 %collective-permute-start.4 = (bf16[256,2048]{1,0:T(8,128)(2,1)S(1)}, bf16[256,2048]{1,0:T(8,128)(2,1)}, u32[]{:S(2)}, u32[]{:S(2)}) collective-permute-start(bf16[256,2048]{1,0:T(8,128)(2,1)S(1)} %copy-done.2), channel_id=1, source_target_pairs={{0,2},{1,3},{2,0},{3,1},{4,6},{5,7},{6,4},{7,5},{8,10},{9,11},{10,... | collective-permute-start | bytes 3145736 | tf_op jit(solution)/shard_map/ppermute | solution.py:9
  37.7 28.5 %all-to-all-start = ((bf16[32,48,256]{2,1,0:T(8,128)(2,1)}), bf16[32,48,256]{2,1,0:T(8,128)(2,1)}, u32[]{:S(2)}, u32[]{:S(2)}) async-start(bf16[32,48,256]{2,1,0:T(8,128)(2,1)} %bitcast.210), calls=%async_computation | async-start | bytes 1572864 | tf_op jit(solution)/shard_map/all_to_all | solution.py:198
  45.2 20.0 %collective-permute-start.3 = (bf16[256,2048]{1,0:T(8,128)(2,1)S(1)}, bf16[256,2048]{1,0:T(8,128)(2,1)S(1)}, u32[]{:S(2)}, u32[]{:S(2)}) collective-permute-start(bf16[256,2048]{1,0:T(8,128)(2,1)S(1)} %copy-done.2), channel_id=1, source_target_pairs={{0,1},{1,0},{2,3},{3,2},{4,5},{5,4},{6,7},{7,6},{8,9},{9,8},{10,11... | collective-permute-start | bytes 3145736 | tf_op jit(solution)/shard_map/ppermute | solution.py:9
  76.6 13.3 %collective-permute-start.6 = (bf16[2,2,2,2,64,1024]{5,4,2,3,0,1:T(8,128)(2,1)}, bf16[2,2,2,2,64,1024]{5,4,2,3,0,1:T(8,128)(2,1)}, u32[]{:S(2)}, u32[]{:S(2)}) collective-permute-start(bf16[2,2,2,2,64,1024]{5,4,2,3,0,1:T(8,128)(2,1)} %bitcast.199), channel_id=1, source_target_pairs={{0,1},{1,0},{2,3},{3,2},{4,5},{5,4},{6,7},{7,6},{8,9},{9,8},{10,11... | collective-permute-start | bytes 6291464 | tf_op jit(solution)/shard_map/ppermute | solution.py:9
  80.1 6.8 %collective-permute-start.7 = (bf16[2,2,2,2,32,1024]{5,4,0,1,2,3:T(8,128)(2,1)}, bf16[2,2,2,2,32,1024]{5,4,0,1,2,3:T(8,128)(2,1)}, u32[]{:S(2)}, u32[]{:S(2)}) collective-permute-start(bf16[2,2,2,2,32,1024]{5,4,0,1,2,3:T(8,128)(2,1)} %bitcast.200), channel_id=1, source_target_pairs={{0,1},{1,0},{2,3},{3,2},{4,5},{5,4},{6,7},{7,6},{8,9},{9,8},{10,11... | collective-permute-start | bytes 3145736 | tf_op jit(solution)/shard_map/ppermute | solution.py:9
  80.1 28.4 %all-to-all-start.1 = ((bf16[32,48,256]{2,1,0:T(8,128)(2,1)}), bf16[32,48,256]{2,1,0:T(8,128)(2,1)}, u32[]{:S(2)}, u32[]{:S(2)}) async-start(bf16[32,48,256]{2,1,0:T(8,128)(2,1)} %bitcast.204), calls=%async_computation.1 | async-start | bytes 1572864 | tf_op jit(solution)/shard_map/all_to_all | solution.py:198
  119.1 16.8 %collective-permute-start.13 = (bf16[2,2,2,32,1024]{4,3,0,1,2:T(8,128)(2,1)S(1)}, bf16[2,2,2,32,1024]{4,3,0,1,2:T(8,128)(2,1)S(1)}, u32[]{:S(2)}, u32[]{:S(2)}) collective-permute-start(bf16[2,2,2,32,1024]{4,3,0,1,2:T(8,128)(2,1)S(1)} %dynamic-slice_bitcast_fusion), channel_id=1, source_target_pairs={{0,2},{1,3},{2,0},{3,1},{4,6},{5,7},{6,4},{7,5},{8,10},{9,11},{10,... | collective-permute-start | bytes 1572872 | tf_op jit(solution)/shard_map/ppermute | solution.py:9
  120.8 14.9 %collective-permute-start.11 = (bf16[2,2,2,32,1024]{4,3,2,0,1:T(8,128)(2,1)S(1)}, bf16[2,2,2,32,1024]{4,3,2,0,1:T(8,128)(2,1)S(1)}, u32[]{:S(2)}, u32[]{:S(2)}) collective-permute-start(bf16[2,2,2,32,1024]{4,3,2,0,1:T(8,128)(2,1)S(1)} %dynamic-slice_bitcast_fusion.2), channel_id=1, source_target_pairs={{0,4},{4,0},{8,12},{12,8},{16,20},{20,16},{24,28},{28,24},{1,5},{5... | collective-permute-start | bytes 1572872 | tf_op jit(solution)/shard_map/ppermute | solution.py:9
  121.8 15.8 %collective-permute-start.12 = (bf16[2,2,2,32,1024]{4,3,1,2,0:T(8,128)(2,1)S(1)}, bf16[2,2,2,32,1024]{4,3,1,2,0:T(8,128)(2,1)S(1)}, u32[]{:S(2)}, u32[]{:S(2)}) collective-permute-start(bf16[2,2,2,32,1024]{4,3,1,2,0:T(8,128)(2,1)S(1)} %dynamic-slice_bitcast_fusion.1), channel_id=1, source_target_pairs={{0,8},{4,12},{8,0},{12,4},{16,24},{20,28},{24,16},{28,20},{1,9},{5... | collective-permute-start | bytes 1572872 | tf_op jit(solution)/shard_map/ppermute | solution.py:9
  124.6 22.3 %collective-permute-start.20 = (bf16[2,2,256,256]{2,3,0,1:T(8,128)(2,1)S(1)}, bf16[2,2,256,256]{2,3,0,1:T(8,128)(2,1)S(1)}, u32[]{:S(2)}, u32[]{:S(2)}) collective-permute-start(bf16[2,2,256,256]{2,3,0,1:T(8,128)(2,1)S(1)} %bitcast.211), channel_id=1, source_target_pairs={{0,4},{4,0},{8,12},{12,8},{16,20},{20,16},{24,28},{28,24},{1,5},{5... | collective-permute-start | bytes 1572872 | tf_op jit(solution)/shard_map/ppermute | solution.py:9
  126.1 12.8 %collective-permute-start.10 = (bf16[256,256]{1,0:T(8,128)(2,1)S(1)}, bf16[256,256]{1,0:T(8,128)(2,1)S(1)}, u32[]{:S(2)}, u32[]{:S(2)}) collective-permute-start(bf16[256,256]{1,0:T(8,128)(2,1)S(1)} %get-tuple-element.84), channel_id=1, source_target_pairs={{0,3},{1,2},{2,1},{3,0},{4,7},{5,6},{6,5},{7,4},{8,11},{9,10},{10,... | collective-permute-start | bytes 393224 | tf_op jit(solution)/shard_map/ppermute | solution.py:9
  135.9 6.0 %collective-permute-start.9 = (bf16[256,256]{1,0:T(8,128)(2,1)S(1)}, bf16[256,256]{1,0:T(8,128)(2,1)S(1)}, u32[]{:S(2)}, u32[]{:S(2)}) collective-permute-start(bf16[256,256]{1,0:T(8,128)(2,1)S(1)} %get-tuple-element.85), channel_id=1, source_target_pairs={{0,2},{1,3},{2,0},{3,1},{4,6},{5,7},{6,4},{7,5},{8,10},{9,11},{10,... | collective-permute-start | bytes 393224 | tf_op jit(solution)/shard_map/ppermute | solution.py:9
  137.9 13.8 %collective-permute-start.16 = (bf16[2,2,32,1024]{3,2,0,1:T(8,128)(2,1)S(1)}, bf16[2,2,32,1024]{3,2,0,1:T(8,128)(2,1)S(1)}, u32[]{:S(2)}, u32[]{:S(2)}) collective-permute-start(bf16[2,2,32,1024]{3,2,0,1:T(8,128)(2,1)S(1)} %dynamic-slice_bitcast_fusion.4), channel_id=1, source_target_pairs={{0,4},{4,0},{8,12},{12,8},{16,20},{20,16},{24,28},{28,24},{1,5},{5... | collective-permute-start | bytes 786440 | tf_op jit(solution)/shard_map/ppermute | solution.py:9
  138.9 14.2 %collective-permute-start.15 = (bf16[2,2,32,1024]{3,2,0,1:T(8,128)(2,1)S(1)}, bf16[2,2,32,1024]{3,2,0,1:T(8,128)(2,1)S(1)}, u32[]{:S(2)}, u32[]{:S(2)}) collective-permute-start(bf16[2,2,32,1024]{3,2,0,1:T(8,128)(2,1)S(1)} %dynamic-slice_bitcast_fusion.5), channel_id=1, source_target_pairs={{0,16},{4,20},{8,24},{12,28},{16,0},{20,4},{24,8},{28,12},{1,17},{... | collective-permute-start | bytes 786440 | tf_op jit(solution)/shard_map/ppermute | solution.py:9
  139.0 12.8 %collective-permute-start.14 = (bf16[2,2,32,1024]{3,2,1,0:T(8,128)(2,1)S(1)}, bf16[2,2,32,1024]{3,2,1,0:T(8,128)(2,1)S(1)}, u32[]{:S(2)}, u32[]{:S(2)}) collective-permute-start(bf16[2,2,32,1024]{3,2,1,0:T(8,128)(2,1)S(1)} %dynamic-slice_bitcast_fusion.6), channel_id=1, source_target_pairs={{0,8},{4,12},{8,0},{12,4},{16,24},{20,28},{24,16},{28,20},{1,9},{5... | collective-permute-start | bytes 786440 | tf_op jit(solution)/shard_map/ppermute | solution.py:9
  153.2 6.7 %collective-permute-start.19 = (bf16[2,32,1024]{2,1,0:T(8,128)(2,1)S(1)}, bf16[2,32,1024]{2,1,0:T(8,128)(2,1)S(1)}, u32[]{:S(2)}, u32[]{:S(2)}) collective-permute-start(bf16[2,32,1024]{2,1,0:T(8,128)(2,1)S(1)} %dynamic-slice_bitcast_fusion.8), channel_id=1, source_target_pairs={{0,8},{4,12},{8,0},{12,4},{16,24},{20,28},{24,16},{28,20},{1,9},{5... | collective-permute-start | bytes 393224 | tf_op jit(solution)/shard_map/ppermute | solution.py:9
  153.3 6.7 %collective-permute-start.18 = (bf16[2,32,1024]{2,1,0:T(8,128)(2,1)S(1)}, bf16[2,32,1024]{2,1,0:T(8,128)(2,1)S(1)}, u32[]{:S(2)}, u32[]{:S(2)}) collective-permute-start(bf16[2,32,1024]{2,1,0:T(8,128)(2,1)S(1)} %dynamic-slice_bitcast_fusion.9), channel_id=1, source_target_pairs={{0,2},{1,3},{2,0},{3,1},{4,6},{5,7},{6,4},{7,5},{8,10},{9,11},{10,... | collective-permute-start | bytes 393224 | tf_op jit(solution)/shard_map/ppermute | solution.py:9
  154.5 8.7 %collective-permute-start.17 = (bf16[2,32,1024]{2,1,0:T(8,128)(2,1)S(1)}, bf16[2,32,1024]{2,1,0:T(8,128)(2,1)S(1)}, u32[]{:S(2)}, u32[]{:S(2)}) collective-permute-start(bf16[2,32,1024]{2,1,0:T(8,128)(2,1)S(1)} %dynamic-slice_bitcast_fusion.10), channel_id=1, source_target_pairs={{0,16},{4,20},{8,24},{12,28},{16,0},{20,4},{24,8},{28,12},{1,17},{... | collective-permute-start | bytes 393224 | tf_op jit(solution)/shard_map/ppermute | solution.py:9
  163.3 8.5 %collective-permute-start.24 = (bf16[2,256,256]{1,2,0:T(8,128)(2,1)S(1)}, bf16[2,256,256]{1,2,0:T(8,128)(2,1)S(1)}, u32[]{:S(2)}, u32[]{:S(2)}) collective-permute-start(bf16[2,256,256]{1,2,0:T(8,128)(2,1)S(1)} %dynamic-slice_bitcast_fusion.3), channel_id=1, source_target_pairs={{0,8},{4,12},{8,0},{12,4},{16,24},{20,28},{24,16},{28,20},{1,9},{5... | collective-permute-start | bytes 786440 | tf_op jit(solution)/shard_map/ppermute | solution.py:9
  163.4 6.2 %collective-permute-start.23 = (bf16[32,1024]{1,0:T(8,128)(2,1)S(1)}, bf16[32,1024]{1,0:T(8,128)(2,1)S(1)}, u32[]{:S(2)}, u32[]{:S(2)}) collective-permute-start(bf16[32,1024]{1,0:T(8,128)(2,1)S(1)} %dynamic-slice_bitcast_fusion.11), channel_id=1, source_target_pairs={{0,16},{4,20},{8,24},{12,28},{16,0},{20,4},{24,8},{28,12},{1,17},{... | collective-permute-start | bytes 196616 | tf_op jit(solution)/shard_map/ppermute | solution.py:9
  171.9 7.3 %collective-permute-start.25 = (bf16[256,256]{0,1:T(8,128)(2,1)S(1)}, bf16[256,256]{0,1:T(8,128)(2,1)S(1)}, u32[]{:S(2)}, u32[]{:S(2)}) collective-permute-start(bf16[256,256]{0,1:T(8,128)(2,1)S(1)} %dynamic-slice_bitcast_fusion.7), channel_id=1, source_target_pairs={{0,16},{4,20},{8,24},{12,28},{16,0},{20,4},{24,8},{28,12},{1,17},{... | collective-permute-start | bytes 393224 | tf_op jit(solution)/shard_map/ppermute | solution.py:9
  (29 other events, 151.0 us)

commit v2 on v1

--- a/solution.py
+++ b/solution.py
@@ -30,6 +30,27 @@
     came = exchange(send, axis_name, 1 << bit)
     value = keep.astype(jnp.float32) + came.astype(jnp.float32)
     return value if last else value.astype(jnp.bfloat16)
+
+
+def fold_last(value, dims):
+    dims = sorted(dims, key=lambda entry: (entry[0] != "ctx", -entry[1]))
+    tp_bits = axis_bits("tp")
+    devices = lax.axis_size("ctx") * lax.axis_size("tp")
+    mine = [(lax.axis_index(axis_name) >> bit) & 1 for axis_name, bit in dims]
+    weights = [1 << (bit + (tp_bits if axis_name == "ctx" else 0)) for axis_name, bit in dims]
+    total = None
+    for first in range(2):
+        for second in range(2):
+            block = lax.dynamic_index_in_dim(value, mine[0] ^ first, 0, keepdims=False)
+            block = lax.dynamic_index_in_dim(block, mine[1] ^ second, 0, keepdims=False)
+            flip = first * weights[0] + second * weights[1]
+            if flip:
+                block = lax.ppermute(
+                    block, ("ctx", "tp"), [(rank, rank ^ flip) for rank in range(devices)]
+                )
+            block = block.astype(jnp.float32)
+            total = block if total is None else total + block
+    return total
 
 
 def split_bits(value, steps):
@@ -239,6 +260,7 @@
         [pick(local_rows, row_of_slot, returned[part]) for part in range(tp_count)], axis=1
     )
     two_grad = rows_product(output_grad, activated).astype(jnp.bfloat16)
+    output_grad, two_grad = lax.optimization_barrier((output_grad, two_grad))
     raised_grad = raised_backward(output_grad, segments, depthwise_taps, pointwise_two, kept_state)
     one_grad = rows_product(raised_grad, normed).astype(jnp.bfloat16)
     all_steps = ctx_steps + tp_steps
@@ -272,13 +294,14 @@
         jnp.dot(held, weights, preferred_element_type=jnp.float32)
         for held, weights in zip(row_blocks, projector_blocks)
     ).astype(jnp.bfloat16)
-    left = len(orders[0]) - len(ctx_steps) + 1
-    for position in range(1, left):
-        parts = lax.optimization_barrier(advance(parts, position))
-    for taken, position in enumerate(range(left, len(orders[0]))):
-        weight = fold_step(weight, ctx_steps[taken:], ctx_steps[taken])
+    count = len(orders[0])
+    for position in range(1, count - 2):
+        taken = position - (count - len(ctx_steps))
+        if taken >= 0:
+            weight = fold_step(weight, ctx_steps[taken:], ctx_steps[taken])
         parts, weight = lax.optimization_barrier((advance(parts, position), weight))
-    projector_grad = fold_step(weight, ctx_steps[-1:], ctx_steps[-1], last=True).T
+    parts = [fold_last(part, order[-2:]) for part, order in zip(parts, orders)]
+    projector_grad = fold_last(weight, ctx_steps[-2:]).T
     one_part = jnp.concatenate(parts[:2], axis=0).T
     two_part = parts[2].T
     return (llm_embed, projector_grad, one_part, two_part)

time: 181 us -> 180 us (level)
  waiting for transfers between devices: 67.5 us -> 60.3 us
  starting transfers between devices: 35.5 us -> 41.9 us
    ppermute x0 -> x12, starting transfers between devices: none -> 16.9 us  [fold_last(): lax.ppermute(block, ('ctx', 'tp'), [(rank, rank ^ flip) for rank in range...]
    ppermute x26 -> x18, waiting for transfers between devices: 53.1 us -> 38.6 us  [exchange(): lax.ppermute(value, axis_name, [(rank, rank ^ flip) for rank in range(siz...]
    ppermute x26 -> x18, starting transfers between devices: 23.6 us -> 13 us  [exchange(): lax.ppermute(value, axis_name, [(rank, rank ^ flip) for rank in range(siz...]
    ppermute x0 -> x12, waiting for transfers between devices: none -> 7.42 us  [fold_last(): lax.ppermute(block, ('ctx', 'tp'), [(rank, rank ^ flip) for rank in range...]
    convert_element_type x13 -> x9, other arithmetic: 6.83 us -> 6.68 us  [fold_step(): return value if last else value.astype(jnp.bfloat16)]
  transfers between devices with their start and end apart: 28 -> 32, of which waited for: 14 -> 12; matrix products, arithmetic and copies ran while one was open for 28% -> 27% of each run, Pallas kernels for 0% -> 0%
where the time goes in v2:
time: 180 us; the launch traced here: 179 us
  waiting for transfers between devices  60.3 us (34%)
  starting transfers between devices  41.9 us (23%)
  matrix products  36.1 us (20%)
  local copies, waits for them, and re-layouts  19.7 us (11%)
  other arithmetic  19.7 us (11%)
    ppermute x18, waiting for transfers between devices, exchange(): lax.ppermute(value, axis_name, [(rank, rank ^ flip) for rank in range(siz...  38.6 us
    ppermute x12, starting transfers between devices, fold_last(): lax.ppermute(block, ('ctx', 'tp'), [(rank, rank ^ flip) for rank in range...  16.9 us
    all_to_all x2, waiting for transfers between devices, spread(): lax.all_to_all(values.reshape(device_count, slot_count, feature_part), ('...  14.4 us
    ppermute x18, starting transfers between devices, exchange(): lax.ppermute(value, axis_name, [(rank, rank ^ flip) for rank in range(siz...  13 us
    all_to_all x2, starting transfers between devices, spread(): lax.all_to_all(values.reshape(device_count, slot_count, feature_part), ('...  12 us
    dot_general x7, matrix products, rows_product(): lax.dot_general(left, right, (((0,), (0,)), ((), ())), preferred_element_...  9.5 us
    ppermute x12, waiting for transfers between devices, fold_last(): lax.ppermute(block, ('ctx', 'tp'), [(rank, rank ^ flip) for rank in range...  7.42 us
    convert_element_type x9, other arithmetic, fold_step(): return value if last else value.astype(jnp.bfloat16)  6.68 us
  transfers between devices with their start and end apart: 32, of which 12 were waited for; matrix products, arithmetic and copies ran while one was open for 27% of the time, Pallas kernels for 0%

profile of v2, /device:TPU:0, one launch (start us, length us, event | category | flops | bytes accessed | tf_op | source)
XLA Modules:
  0.0 179.1 jit_solution(6071362169845936760)
XLA Ops:
  0.6 3.1 %collective-permute-start.1 = (bf16[256,2048]{1,0:T(8,128)(2,1)}, bf16[256,2048]{1,0:T(8,128)(2,1)}, u32[]{:S(2)}, u32[]{:S(2)}) collective-permute-start(bf16[256,2048]{1,0:T(8,128)(2,1)} %param.25), channel_id=1, source_target_pairs={{0,2},{1,3},{2,0},{3,1},{4,6},{5,7},{6,4},{7,5},{8,10},{9,11},{10,... | collective-permute-start | bytes 3145736 | tf_op jit(solution)/shard_map/ppermute | solution.py:9
  12.9 2.2 %compare_convert_fusion = bf16[1024,1536]{1,0:T(8,128)(2,1)} fusion(s32[1536]{0:T(1024)S(1)} %select_n.151, s32[1024]{0:T(1024)S(1)} %pad_add_fusion), kind=kLoop, calls=%fused_computation | loop fusion | flops 3145728 | bytes 3155968 | tf_op jit(solution)/shard_map/convert_element_type | solution.py:237
  15.6 3.5 %fusion.114 = f32[256,2048]{1,0:T(8,128)S(1)} fusion(bf16[1024,2048]{1,0:T(8,128)(2,1)} %param.21, f32[256,1024]{1,0:T(8,128)S(1)} %get-tuple-element.119, f32[1024]{0:T(1024)S(1)} %convert_element_type.399, f32[256]{0:T(256)S(1)} %add_rsqrt_fusion, f32[256]{0:T(256)S(1)} %broadcast_multiply_fusion.8), kind=kOutput, calls=%fused_computation.252 | convolution fusion | flops 1074790400 | bytes 7346176 | tf_op jit(solution)/shard_map/dot_general | solution.py:123
  22.0 5.2 %collective-permute-done.1 = bf16[256,2048]{1,0:T(8,128)(2,1)} collective-permute-done((bf16[256,2048]{1,0:T(8,128)(2,1)}, bf16[256,2048]{1,0:T(8,128)(2,1)}, u32[]{:S(2)}, u32[]{:S(2)}) %collective-permute-start.1) | collective-permute-done | bytes 1048608 | tf_op jit(solution)/shard_map/ppermute | solution.py:9
  27.3 2.6 %multiply_add_fusion = f32[256,1024]{1,0:T(8,128)} fusion(f32[256,1024]{1,0:T(8,128)S(1)} %slice_multiply_fusion.2, f32[256]{0:T(256)S(1)} %get-tuple-element.117, f32[1024]{0:T(1024)S(1)} %bitcast.231, f32[256]{0:T(256)S(1)} %get-tuple-element.111, f32[1024]{0:T(1024)S(1)} %bitcast.229, f32[256]{0:T(256)S(1)} %get-tuple-element.112, f32[1024]{0:T(1024)S(1)} %bitcast.227, ...), kind=kLoop, calls=%fused_computation.92 | loop fusion | flops 6553600 | bytes 2142208 | tf_op jit(solution)/shard_map/add | solution.py:97
  35.7 1.9 %convolution_convert_fusion.1 = bf16[1536,256]{1,0:T(8,128)(2,1)} fusion(bf16[1024,1536]{1,0:T(8,128)(2,1)S(1)} %copy-done.16, bf16[256,256]{1,0:T(8,128)(2,1)S(1)} %convolution_convert_fusion.12, bf16[256,256]{1,0:T(8,128)(2,1)S(1)} %convolution_convert_fusion.13, bf16[256,256]{1,0:T(8,128)(2,1)S(1)} %convolution_convert_fusion.14, ...), kind=kOutput, calls=%fused_computation.13 | convolution fusion | flops 807796736 | bytes 4456448 | tf_op jit(solution)/shard_map/dot_general | solution.py:154
  37.6 5.2 %all-to-all-start = ((bf16[32,48,256]{2,1,0:T(8,128)(2,1)}), bf16[32,48,256]{2,1,0:T(8,128)(2,1)}, u32[]{:S(2)}, u32[]{:S(2)}) async-start(bf16[32,48,256]{2,1,0:T(8,128)(2,1)} %bitcast.208), calls=%async_computation | async-start | bytes 1572864 | tf_op jit(solution)/shard_map/all_to_all | solution.py:219
  42.9 2.3 %fusion.8 = bf16[256,1024]{1,0:T(8,128)(2,1)S(1)} fusion(f32[256,1024]{1,0:T(8,128)} %copy-done.9, bf16[1024,1024]{1,0:T(8,128)(2,1)S(1)} %copy-done, f32[256,1024]{1,0:T(8,128)} %multiply_add_fusion), kind=kOutput, calls=%fused_computation.24 | convolution fusion | flops 538705920 | bytes 4718592 | tf_op jit(solution)/shard_map/dot_general | solution.py:129
  45.2 17.9 %collective-permute-done.4 = bf16[256,2048]{1,0:T(8,128)(2,1)} collective-permute-done((bf16[256,2048]{1,0:T(8,128)(2,1)S(1)}, bf16[256,2048]{1,0:T(8,128)(2,1)}, u32[]{:S(2)}, u32[]{:S(2)}) %collective-permute-start.4) | collective-permute-done | bytes 1048608 | tf_op jit(solution)/shard_map/ppermute | solution.py:9
  80.3 6.8 %all-to-all-start.1 = ((bf16[32,48,256]{2,1,0:T(8,128)(2,1)}), bf16[32,48,256]{2,1,0:T(8,128)(2,1)}, u32[]{:S(2)}, u32[]{:S(2)}) async-start(bf16[32,48,256]{2,1,0:T(8,128)(2,1)} %bitcast.202), calls=%async_computation.1 | async-start | bytes 1572864 | tf_op jit(solution)/shard_map/all_to_all | solution.py:219
  87.1 2.9 %fusion.7 = bf16[2,2,2,2,32,1024]{5,4,1,0,2,3:T(8,128)(2,1)} fusion(bf16[2,2,2,2,32,1024]{5,4,1,0,2,3:T(8,128)(2,1)} %collective-permute-done.7, bf16[2,2,2,2,1,32,1024]{6,5,4,3,2,1,0:T(8,128)(2,1)} %get-tuple-element.58), kind=kLoop, calls=%fused_computation.18 | loop fusion | flops 2097152 | bytes 3145728 | tf_op jit(solution)/shard_map/convert_element_type | solution.py:32
  90.1 2.7 %fusion = bf16[2,2,2,2,64,1024]{5,4,3,2,0,1:T(8,128)(2,1)S(1)} fusion(bf16[2,2,2,2,64,1024]{5,4,3,2,0,1:T(8,128)(2,1)} %collective-permute-done.6, bf16[2,2,2,2,1,64,1024]{6,5,4,3,2,1,0:T(8,128)(2,1)S(1)} %get-tuple-element.54), kind=kLoop, calls=%fused_computation.2 | loop fusion | flops 4194304 | bytes 6291456 | tf_op jit(solution)/shard_map/convert_element_type | solution.py:32
  94.3 14.4 %all-to-all-done.1 = bf16[32,48,256]{2,1,0:T(8,128)(2,1)} async-done(((bf16[32,48,256]{2,1,0:T(8,128)(2,1)}), bf16[32,48,256]{2,1,0:T(8,128)(2,1)}, u32[]{:S(2)}, u32[]{:S(2)}) %all-to-all-start.1) | async-done | bytes 786464 | tf_op jit(solution)/shard_map/all_to_all | solution.py:219
  108.7 3.1 %convolution_convert_fusion.3 = bf16[1024,256]{1,0:T(8,128)(2,1)S(1)} fusion(bf16[1024,1536]{1,0:T(8,128)(2,1)} %compare_convert_fusion, bf16[1536,256]{1,0:T(8,128)(2,1)} %bitcast.36), kind=kOutput, calls=%fused_computation.26 | convolution fusion | flops 805568512 | bytes 4456448 | tf_op jit(solution)/shard_map/dot_general | solution.py:283
  117.2 1.9 %reshape.332 = bf16[2,2,2,256,256]{3,2,1,0,4:T(2,128)(2,1)S(1)} reshape(bf16[2048,256]{0,1:T(8,128)(2,1)} %fusion.6) | data formatting | bytes 2097152 | tf_op jit(solution)/shard_map/reshape | solution.py:57
  122.4 2.2 %constant_dynamic-slice_fusion.1 = (bf16[2,2,1,256,256]{3,2,1,0,4:T(2,128)(2,1)S(1)}, bf16[2,2,1,256,256]{3,2,1,0,4:T(2,128)(2,1)S(1)}) fusion(bf16[2,2,2,256,256]{3,2,1,0,4:T(2,128)(2,1)S(1)} %reshape.332, s32[]{:T(128)S(6)} %select_n.158, s32[]{:T(128)S(6)} %select_n.159), kind=kLoop, calls=%fused_computation.204 | loop fusion | bytes 2097160 | tf_op jit(solution)/shard_map/jit(dynamic_index_in_dim)/dynamic_slice | solution.py:28
  126.3 7.8 %collective-permute-done.13 = bf16[2,2,2,32,1024]{4,3,1,0,2:T(8,128)(2,1)S(1)} collective-permute-done((bf16[2,2,2,32,1024]{4,3,1,0,2:T(8,128)(2,1)S(1)}, bf16[2,2,2,32,1024]{4,3,1,0,2:T(8,128)(2,1)S(1)}, u32[]{:S(2)}, u32[]{:S(2)}) %collective-permute-start.13) | collective-permute-done | bytes 524320 | tf_op jit(solution)/shard_map/ppermute | solution.py:9
  145.7 2.1 %collective-permute-done.17 = bf16[2,2,256,256]{2,3,1,0:T(8,128)(2,1)S(1)} collective-permute-done((bf16[2,2,256,256]{2,3,1,0:T(8,128)(2,1)S(1)}, bf16[2,2,256,256]{2,3,1,0:T(8,128)(2,1)S(1)}, u32[]{:S(2)}, u32[]{:S(2)}) %collective-permute-start.17) | collective-permute-done | bytes 524320 | tf_op jit(solution)/shard_map/ppermute | solution.py:9
  148.0 4.1 %collective-permute-done.16 = bf16[2,2,32,1024]{3,2,1,0:T(8,128)(2,1)S(1)} collective-permute-done((bf16[2,2,32,1024]{3,2,1,0:T(8,128)(2,1)S(1)}, bf16[2,2,32,1024]{3,2,1,0:T(8,128)(2,1)S(1)}, u32[]{:S(2)}, u32[]{:S(2)}) %collective-permute-start.16) | collective-permute-done | bytes 262176 | tf_op jit(solution)/shard_map/ppermute | solution.py:9
  154.6 2.2 %collective-permute-start.29 = (bf16[32,1024]{1,0:T(8,128)(2,1)S(1)}, bf16[32,1024]{1,0:T(8,128)(2,1)S(1)}, u32[]{:S(2)}, u32[]{:S(2)}) collective-permute-start(bf16[32,1024]{1,0:T(8,128)(2,1)S(1)} %get-tuple-element.82), channel_id=1, source_target_pairs={{0,24},{1,25},{2,26},{3,27},{4,28},{5,29},{6,30},{7,31},{8,16},{9,... | collective-permute-start | bytes 196616 | tf_op jit(solution)/shard_map/ppermute | solution.py:48
  158.6 2.9 %collective-permute-start.23 = (bf16[32,1024]{1,0:T(8,128)(2,1)S(1)}, bf16[32,1024]{1,0:T(8,128)(2,1)S(1)}, u32[]{:S(2)}, u32[]{:S(2)}) collective-permute-start(bf16[32,1024]{1,0:T(8,128)(2,1)S(1)} %get-tuple-element.85), channel_id=1, source_target_pairs={{0,18},{1,19},{2,16},{3,17},{4,22},{5,23},{6,20},{7,21},{8,26},{9,... | collective-permute-start | bytes 196616 | tf_op jit(solution)/shard_map/ppermute | solution.py:48
  161.5 2.1 %collective-permute-done.28 = bf16[32,1024]{1,0:T(8,128)(2,1)S(1)} collective-permute-done((bf16[32,1024]{1,0:T(8,128)(2,1)S(1)}, bf16[32,1024]{1,0:T(8,128)(2,1)S(1)}, u32[]{:S(2)}, u32[]{:S(2)}) %collective-permute-start.28) | collective-permute-done | bytes 65568 | tf_op jit(solution)/shard_map/ppermute | solution.py:48
  170.1 2.2 %collective-permute-start.20 = (bf16[256,256]{0,1:T(8,128)(2,1)S(1)}, bf16[256,256]{0,1:T(8,128)(2,1)S(1)}, u32[]{:S(2)}, u32[]{:S(2)}) collective-permute-start(bf16[256,256]{0,1:T(8,128)(2,1)S(1)} %get-tuple-element.75), channel_id=1, source_target_pairs={{0,24},{1,25},{2,26},{3,27},{4,28},{5,29},{6,30},{7,31},{8,16},{9,... | collective-permute-start | bytes 393224 | tf_op jit(solution)/shard_map/ppermute | solution.py:48
  174.8 3.5 %collective-permute-done.19 = bf16[256,256]{0,1:T(8,128)(2,1)S(1)} collective-permute-done((bf16[256,256]{0,1:T(8,128)(2,1)S(1)}, bf16[256,256]{0,1:T(8,128)(2,1)S(1)}, u32[]{:S(2)}, u32[]{:S(2)}) %collective-permute-start.19) | collective-permute-done | bytes 131104 | tf_op jit(solution)/shard_map/ppermute | solution.py:48
  (191 shorter events, 72.7 us)
Async XLA Ops:
  0.6 26.5 %collective-permute-start.1 = (bf16[256,2048]{1,0:T(8,128)(2,1)}, bf16[256,2048]{1,0:T(8,128)(2,1)}, u32[]{:S(2)}, u32[]{:S(2)}) collective-permute-start(bf16[256,2048]{1,0:T(8,128)(2,1)} %param.25), channel_id=1, source_target_pairs={{0,2},{1,3},{2,0},{3,1},{4,6},{5,7},{6,4},{7,5},{8,10},{9,11},{10,... | collective-permute-start | bytes 3145736 | tf_op jit(solution)/shard_map/ppermute | solution.py:9
  3.7 29.6 %collective-permute-start = (bf16[256,2048]{1,0:T(8,128)(2,1)}, bf16[256,2048]{1,0:T(8,128)(2,1)}, u32[]{:S(2)}, u32[]{:S(2)}) collective-permute-start(bf16[256,2048]{1,0:T(8,128)(2,1)} %param.25), channel_id=1, source_target_pairs={{0,1},{1,0},{2,3},{3,2},{4,5},{5,4},{6,7},{7,6},{8,9},{9,8},{10,11... | collective-permute-start | bytes 3145736 | tf_op jit(solution)/shard_map/ppermute | solution.py:9
  27.2 8.0 %collective-permute-start.2 = (bf16[256,2048]{1,0:T(8,128)(2,1)}, bf16[256,2048]{1,0:T(8,128)(2,1)S(1)}, u32[]{:S(2)}, u32[]{:S(2)}) collective-permute-start(bf16[256,2048]{1,0:T(8,128)(2,1)} %collective-permute-done.1), channel_id=1, source_target_pairs={{0,1},{1,0},{2,3},{3,2},{4,5},{5,4},{6,7},{7,6},{8,9},{9,8},{10,11... | collective-permute-start | bytes 3145736 | tf_op jit(solution)/shard_map/ppermute | solution.py:9
  29.9 33.2 %collective-permute-start.4 = (bf16[256,2048]{1,0:T(8,128)(2,1)S(1)}, bf16[256,2048]{1,0:T(8,128)(2,1)}, u32[]{:S(2)}, u32[]{:S(2)}) collective-permute-start(bf16[256,2048]{1,0:T(8,128)(2,1)S(1)} %copy-done.2), channel_id=1, source_target_pairs={{0,2},{1,3},{2,0},{3,1},{4,6},{5,7},{6,4},{7,5},{8,10},{9,11},{10,... | collective-permute-start | bytes 3145736 | tf_op jit(solution)/shard_map/ppermute | solution.py:9
  37.6 28.6 %all-to-all-start = ((bf16[32,48,256]{2,1,0:T(8,128)(2,1)}), bf16[32,48,256]{2,1,0:T(8,128)(2,1)}, u32[]{:S(2)}, u32[]{:S(2)}) async-start(bf16[32,48,256]{2,1,0:T(8,128)(2,1)} %bitcast.208), calls=%async_computation | async-start | bytes 1572864 | tf_op jit(solution)/shard_map/all_to_all | solution.py:219
  45.1 20.0 %collective-permute-start.3 = (bf16[256,2048]{1,0:T(8,128)(2,1)S(1)}, bf16[256,2048]{1,0:T(8,128)(2,1)S(1)}, u32[]{:S(2)}, u32[]{:S(2)}) collective-permute-start(bf16[256,2048]{1,0:T(8,128)(2,1)S(1)} %copy-done.2), channel_id=1, source_target_pairs={{0,1},{1,0},{2,3},{3,2},{4,5},{5,4},{6,7},{7,6},{8,9},{9,8},{10,11... | collective-permute-start | bytes 3145736 | tf_op jit(solution)/shard_map/ppermute | solution.py:9
  77.5 12.6 %collective-permute-start.6 = (bf16[2,2,2,2,64,1024]{5,4,3,2,0,1:T(8,128)(2,1)}, bf16[2,2,2,2,64,1024]{5,4,3,2,0,1:T(8,128)(2,1)}, u32[]{:S(2)}, u32[]{:S(2)}) collective-permute-start(bf16[2,2,2,2,64,1024]{5,4,3,2,0,1:T(8,128)(2,1)} %bitcast.197), channel_id=1, source_target_pairs={{0,1},{1,0},{2,3},{3,2},{4,5},{5,4},{6,7},{7,6},{8,9},{9,8},{10,11... | collective-permute-start | bytes 6291464 | tf_op jit(solution)/shard_map/ppermute | solution.py:9
  80.3 28.4 %all-to-all-start.1 = ((bf16[32,48,256]{2,1,0:T(8,128)(2,1)}), bf16[32,48,256]{2,1,0:T(8,128)(2,1)}, u32[]{:S(2)}, u32[]{:S(2)}) async-start(bf16[32,48,256]{2,1,0:T(8,128)(2,1)} %bitcast.202), calls=%async_computation.1 | async-start | bytes 1572864 | tf_op jit(solution)/shard_map/all_to_all | solution.py:219
  119.2 14.9 %collective-permute-start.13 = (bf16[2,2,2,32,1024]{4,3,1,0,2:T(8,128)(2,1)S(1)}, bf16[2,2,2,32,1024]{4,3,1,0,2:T(8,128)(2,1)S(1)}, u32[]{:S(2)}, u32[]{:S(2)}) collective-permute-start(bf16[2,2,2,32,1024]{4,3,1,0,2:T(8,128)(2,1)S(1)} %dynamic-slice_bitcast_fusion), channel_id=1, source_target_pairs={{0,2},{1,3},{2,0},{3,1},{4,6},{5,7},{6,4},{7,5},{8,10},{9,11},{10,... | collective-permute-start | bytes 1572872 | tf_op jit(solution)/shard_map/ppermute | solution.py:9
  120.9 14.0 %collective-permute-start.12 = (bf16[2,2,2,32,1024]{4,3,2,1,0:T(8,128)(2,1)S(1)}, bf16[2,2,2,32,1024]{4,3,2,1,0:T(8,128)(2,1)S(1)}, u32[]{:S(2)}, u32[]{:S(2)}) collective-permute-start(bf16[2,2,2,32,1024]{4,3,2,1,0:T(8,128)(2,1)S(1)} %dynamic-slice_bitcast_fusion.1), channel_id=1, source_target_pairs={{0,8},{4,12},{8,0},{12,4},{16,24},{20,28},{24,16},{28,20},{1,9},{5... | collective-permute-start | bytes 1572872 | tf_op jit(solution)/shard_map/ppermute | solution.py:9
  121.7 14.9 %collective-permute-start.11 = (bf16[2,2,2,32,1024]{4,3,2,0,1:T(8,128)(2,1)S(1)}, bf16[2,2,2,32,1024]{4,3,2,0,1:T(8,128)(2,1)S(1)}, u32[]{:S(2)}, u32[]{:S(2)}) collective-permute-start(bf16[2,2,2,32,1024]{4,3,2,0,1:T(8,128)(2,1)S(1)} %dynamic-slice_bitcast_fusion.2), channel_id=1, source_target_pairs={{0,4},{4,0},{8,12},{12,8},{16,20},{20,16},{24,28},{28,24},{1,5},{5... | collective-permute-start | bytes 1572872 | tf_op jit(solution)/shard_map/ppermute | solution.py:9
  124.7 23.1 %collective-permute-start.17 = (bf16[2,2,256,256]{2,3,1,0:T(8,128)(2,1)S(1)}, bf16[2,2,256,256]{2,3,1,0:T(8,128)(2,1)S(1)}, u32[]{:S(2)}, u32[]{:S(2)}) collective-permute-start(bf16[2,2,256,256]{2,3,1,0:T(8,128)(2,1)S(1)} %bitcast.209), channel_id=1, source_target_pairs={{0,4},{4,0},{8,12},{12,8},{16,20},{20,16},{24,28},{28,24},{1,5},{5... | collective-permute-start | bytes 1572872 | tf_op jit(solution)/shard_map/ppermute | solution.py:9
  126.2 11.4 %collective-permute-start.10 = (bf16[256,256]{1,0:T(8,128)(2,1)S(1)}, bf16[256,256]{1,0:T(8,128)(2,1)S(1)}, u32[]{:S(2)}, u32[]{:S(2)}) collective-permute-start(bf16[256,256]{1,0:T(8,128)(2,1)S(1)} %get-tuple-element.77), channel_id=1, source_target_pairs={{0,3},{1,2},{2,1},{3,0},{4,7},{5,6},{6,5},{7,4},{8,11},{9,10},{10,... | collective-permute-start | bytes 393224 | tf_op jit(solution)/shard_map/ppermute | solution.py:9
  136.8 15.3 %collective-permute-start.16 = (bf16[2,2,32,1024]{3,2,1,0:T(8,128)(2,1)S(1)}, bf16[2,2,32,1024]{3,2,1,0:T(8,128)(2,1)S(1)}, u32[]{:S(2)}, u32[]{:S(2)}) collective-permute-start(bf16[2,2,32,1024]{3,2,1,0:T(8,128)(2,1)S(1)} %dynamic-slice_bitcast_fusion.3), channel_id=1, source_target_pairs={{0,4},{4,0},{8,12},{12,8},{16,20},{20,16},{24,28},{28,24},{1,5},{5... | collective-permute-start | bytes 786440 | tf_op jit(solution)/shard_map/ppermute | solution.py:9
  137.6 14.6 %collective-permute-start.15 = (bf16[2,2,32,1024]{3,2,1,0:T(8,128)(2,1)S(1)}, bf16[2,2,32,1024]{3,2,1,0:T(8,128)(2,1)S(1)}, u32[]{:S(2)}, u32[]{:S(2)}) collective-permute-start(bf16[2,2,32,1024]{3,2,1,0:T(8,128)(2,1)S(1)} %dynamic-slice_bitcast_fusion.4), channel_id=1, source_target_pairs={{0,16},{4,20},{8,24},{12,28},{16,0},{20,4},{24,8},{28,12},{1,17},{... | collective-permute-start | bytes 786440 | tf_op jit(solution)/shard_map/ppermute | solution.py:9
  139.1 13.1 %collective-permute-start.14 = (bf16[2,2,32,1024]{3,2,1,0:T(8,128)(2,1)S(1)}, bf16[2,2,32,1024]{3,2,1,0:T(8,128)(2,1)S(1)}, u32[]{:S(2)}, u32[]{:S(2)}) collective-permute-start(bf16[2,2,32,1024]{3,2,1,0:T(8,128)(2,1)S(1)} %dynamic-slice_bitcast_fusion.5), channel_id=1, source_target_pairs={{0,8},{4,12},{8,0},{12,4},{16,24},{20,28},{24,16},{28,20},{1,9},{5... | collective-permute-start | bytes 786440 | tf_op jit(solution)/shard_map/ppermute | solution.py:9
  154.1 9.5 %collective-permute-start.28 = (bf16[32,1024]{1,0:T(8,128)(2,1)S(1)}, bf16[32,1024]{1,0:T(8,128)(2,1)S(1)}, u32[]{:S(2)}, u32[]{:S(2)}) collective-permute-start(bf16[32,1024]{1,0:T(8,128)(2,1)S(1)} %get-tuple-element.83), channel_id=1, source_target_pairs={{0,16},{1,17},{2,18},{3,19},{4,20},{5,21},{6,22},{7,23},{8,24},{9,... | collective-permute-start | bytes 196616 | tf_op jit(solution)/shard_map/ppermute | solution.py:48
  154.6 9.0 %collective-permute-start.29 = (bf16[32,1024]{1,0:T(8,128)(2,1)S(1)}, bf16[32,1024]{1,0:T(8,128)(2,1)S(1)}, u32[]{:S(2)}, u32[]{:S(2)}) collective-permute-start(bf16[32,1024]{1,0:T(8,128)(2,1)S(1)} %get-tuple-element.82), channel_id=1, source_target_pairs={{0,24},{1,25},{2,26},{3,27},{4,28},{5,29},{6,30},{7,31},{8,16},{9,... | collective-permute-start | bytes 196616 | tf_op jit(solution)/shard_map/ppermute | solution.py:48
  156.9 9.3 %collective-permute-start.21 = (bf16[32,1024]{1,0:T(8,128)(2,1)S(1)}, bf16[32,1024]{1,0:T(8,128)(2,1)S(1)}, u32[]{:S(2)}, u32[]{:S(2)}) collective-permute-start(bf16[32,1024]{1,0:T(8,128)(2,1)S(1)} %get-tuple-element.84), channel_id=1, source_target_pairs={{0,2},{1,3},{2,0},{3,1},{4,6},{5,7},{6,4},{7,5},{8,10},{9,11},{10,... | collective-permute-start | bytes 196616 | tf_op jit(solution)/shard_map/ppermute | solution.py:48
  158.4 9.4 %collective-permute-start.22 = (bf16[32,1024]{1,0:T(8,128)(2,1)S(1)}, bf16[32,1024]{1,0:T(8,128)(2,1)S(1)}, u32[]{:S(2)}, u32[]{:S(2)}) collective-permute-start(bf16[32,1024]{1,0:T(8,128)(2,1)S(1)} %get-tuple-element.86), channel_id=1, source_target_pairs={{0,16},{1,17},{2,18},{3,19},{4,20},{5,21},{6,22},{7,23},{8,24},{9,... | collective-permute-start | bytes 196616 | tf_op jit(solution)/shard_map/ppermute | solution.py:48
  158.6 9.7 %collective-permute-start.23 = (bf16[32,1024]{1,0:T(8,128)(2,1)S(1)}, bf16[32,1024]{1,0:T(8,128)(2,1)S(1)}, u32[]{:S(2)}, u32[]{:S(2)}) collective-permute-start(bf16[32,1024]{1,0:T(8,128)(2,1)S(1)} %get-tuple-element.85), channel_id=1, source_target_pairs={{0,18},{1,19},{2,16},{3,17},{4,22},{5,23},{6,20},{7,21},{8,26},{9,... | collective-permute-start | bytes 196616 | tf_op jit(solution)/shard_map/ppermute | solution.py:48
  163.6 8.7 %collective-permute-start.25 = (bf16[32,1024]{1,0:T(8,128)(2,1)S(1)}, bf16[32,1024]{1,0:T(8,128)(2,1)S(1)}, u32[]{:S(2)}, u32[]{:S(2)}) collective-permute-start(bf16[32,1024]{1,0:T(8,128)(2,1)S(1)} %get-tuple-element.89), channel_id=1, source_target_pairs={{0,4},{1,5},{2,6},{3,7},{4,0},{5,1},{6,2},{7,3},{8,12},{9,13},{10,... | collective-permute-start | bytes 196616 | tf_op jit(solution)/shard_map/ppermute | solution.py:48
  168.2 10.1 %collective-permute-start.19 = (bf16[256,256]{0,1:T(8,128)(2,1)S(1)}, bf16[256,256]{0,1:T(8,128)(2,1)S(1)}, u32[]{:S(2)}, u32[]{:S(2)}) collective-permute-start(bf16[256,256]{0,1:T(8,128)(2,1)S(1)} %get-tuple-element.76), channel_id=1, source_target_pairs={{0,16},{1,17},{2,18},{3,19},{4,20},{5,21},{6,22},{7,23},{8,24},{9,... | collective-permute-start | bytes 393224 | tf_op jit(solution)/shard_map/ppermute | solution.py:48
  170.1 8.3 %collective-permute-start.20 = (bf16[256,256]{0,1:T(8,128)(2,1)S(1)}, bf16[256,256]{0,1:T(8,128)(2,1)S(1)}, u32[]{:S(2)}, u32[]{:S(2)}) collective-permute-start(bf16[256,256]{0,1:T(8,128)(2,1)S(1)} %get-tuple-element.75), channel_id=1, source_target_pairs={{0,24},{1,25},{2,26},{3,27},{4,28},{5,29},{6,30},{7,31},{8,16},{9,... | collective-permute-start | bytes 393224 | tf_op jit(solution)/shard_map/ppermute | solution.py:48
  (33 other events, 198.0 us)
